TPU v7x, 32 devices: a whole 2x2x4 slice. The times are simulated.
32 devices in a mesh: cuts: 8 (over z, x), space: 4 (over y, core).
Axes of the slice: x: 2, y: 2, z: 4, core: 2. Of those that a mesh axis runs over, the one named last changes fastest.
Arguments:
- start_old: float32 [8, 16, 2, 2048], P('cuts', None, None, 'space'), may hold values from -3 to 3
- scales: float32 [8, 2, 2048], P('cuts', None, 'space'), may hold values from 0.92 to 1
- propagator: bfloat16 [2, 2048, 2, 2048], P(None, 'space'), may hold values from -1.2 to 1.2
- pipe_of_cell: int32 [8192], P('space'), may hold values from 0 to 127
- friction: float32 [128], replicated, may hold values from 0.02 to 0.2
Outputs:
- end_new: float32 [8, 16, 2, 2048], P('cuts', None, None, 'space')
All inputs are finite; a program needn't handle non-finite values.
Results may differ from a plain program's by a relative error of at most 0.0048.
Values may be sent and summed in bfloat16 or wider, within the bound.
A program may use at most 64 MiB of HBM per device.

v0:
```python
import jax
import jax.numpy as jnp
from jax import lax
from jax.sharding import PartitionSpec as P

REFINE = 4
STEPS = 16


def with_halo(x, sides, width):
    for axis, dim in sides:
        devices, length = (lax.axis_size(axis), x.shape[dim])
        up = [(i, (i + 1) % devices) for i in range(devices - 1)]
        down = [(j, i) for i, j in up]
        last = lax.slice_in_dim(x, length - width, length, axis=dim)
        leading = lax.slice_in_dim(x, 0, width, axis=dim)
        before = lax.ppermute(last, axis, up)
        after = lax.ppermute(leading, axis, down)
        x = jnp.concatenate([before, x, after], axis=dim)
    return x


def shifted(value, axis, steps):
    count = lax.axis_size(axis)
    leading, last = (max(0, -steps), min(count, count - steps))
    return lax.ppermute(value, axis, [(source, source + steps) for source in range(leading, last)])


def moc_step(head, flow, rate):
    hleft, hright = (head[..., :-2], head[..., 2:])
    qleft, qright = (flow[..., :-2], flow[..., 2:])
    plus = hleft + qleft - rate * qleft * jnp.abs(qleft)
    minus = hright - qright + rate * qright * jnp.abs(qright)
    return (0.5 * (plus + minus), 0.5 * (plus - minus))


def fold_rows(piece, propagator):
    return jnp.einsum("fiqj,bqj->bfi", propagator, piece, preferred_element_type=jnp.float32)


def local(start_old, scales, propagator, pipe_of_cell, friction):
    local_start = start_old[0]
    local_scale = scales[0]
    scen_count = local_start.shape[0]
    coarse_local = local_start.shape[2]
    cells = pipe_of_cell.shape[0]
    pipe_ids = lax.broadcasted_iota(jnp.int32, (cells, friction.shape[0]), 1)
    rate = jnp.sum(jnp.where(pipe_of_cell[:, None] == pipe_ids, friction[None, :], 0.0), axis=1)
    field = jnp.repeat(local_start, REFINE, axis=-1)
    for step in range(STEPS):
        padded = with_halo(field, (("space", 2),), 1)
        head, flow = moc_step(padded[:, 0], padded[:, 1], rate)
        field = jnp.stack([head, flow], axis=1)
    fine_coarse = jnp.mean(field.reshape(scen_count, 2, coarse_local, REFINE), axis=-1)

    def add_piece(piece):
        return fold_rows(piece, propagator)

    old_scaled = (local_scale[None] * local_start).astype(jnp.bfloat16)
    old_image = add_piece(lax.all_gather(old_scaled, "space", axis=2, tiled=True))
    delta = fine_coarse - old_image
    ending = old_image + delta
    first = lax.axis_index("cuts") == 0

    def turn_receive(count, current):
        arrived = shifted(current, "cuts", 1)
        scaled = (local_scale[None] * arrived).astype(jnp.bfloat16)
        image = add_piece(lax.all_gather(scaled, "space", axis=2, tiled=True))
        return jnp.where(first, current, image + delta)

    ending = lax.fori_loop(0, lax.axis_size("cuts") - 1, turn_receive, ending)
    return ending[None]


def solution(mesh):
    placed = (
        P("cuts", None, None, "space"),
        P("cuts", None, "space"),
        P(None, "space", None, None),
        P("space"),
        P(),
    )
    return jax.shard_map(
        local, mesh=mesh, in_specs=placed, out_specs=P("cuts", None, None, "space"), check_vma=False
    )
```

profile of v0, /device:TPU:26, one launch (start us, length us, event | category | flops | bytes accessed | tf_op | source)
XLA Modules:
  0.0 273.0 jit_solution(14311933111800627246)
XLA Ops:
  1.4 1.3 collective-permute-start.2
  2.7 3.0 %collective-permute-start.1 = (f32[16,2,1]{0,2,1:T(1,128)S(1)}, f32[16,2,1]{0,2,1:T(1,128)S(1)}, u32[]{:S(2)}, u32[]{:S(2)}) collective-permute-start(f32[16,2,1]{0,2,1:T(1,128)S(1)} %get-tuple-element.75), channel_id=1, source_target_pairs={{0,1},{1,2},{2,3},{4,5},{5,6},{6,7},{8,9},{9,10},{10,11},{12,13},{... | collective-permute-start | bytes 392 | tf_op jit(solution)/shard_map/ppermute | solution.py:17
  7.2 5.6 %all_gather.6 = bf16[16,2,2048]{2,0,1:T(8,128)(2,1)S(1)} all-gather(bf16[16,2,512]{2,0,1:T(8,128)(2,1)S(1)} %fusion.36), channel_id=1, replica_groups=mesh['cuts'=8,'space'=4] {'space'}, dimensions={2}, use_global_device_ids=true | all-gather | bytes 163840 | tf_op jit(solution)/shard_map/all_gather | solution.py:60
  12.8 1.3 select_reduce_fusion
  14.2 10.7 %copy.32 = bf16[2,512,2,2048]{3,1,2,0:T(8,128)(2,1)} copy(bf16[2,512,2,2048]{3,2,1,0:T(2,128)(2,1)} %param.9) | data formatting | bytes 16777216 | tf_op args[2]
  25.4 1.3 collective-permute-start.4
  26.7 3.0 %collective-permute-start.3 = (f32[16,2,1]{2,0,1:T(8,128)S(1)}, f32[16,2,1]{2,0,1:T(8,128)S(1)}, u32[]{:S(2)}, u32[]{:S(2)}) collective-permute-start(f32[16,2,1]{2,0,1:T(8,128)S(1)} %get-tuple-element.169), channel_id=1, source_target_pairs={{0,1},{1,2},{2,3},{4,5},{5,6},{6,7},{8,9},{9,10},{10,11},{12,13},{... | collective-permute-start | bytes 392 | tf_op jit(solution)/shard_map/ppermute | solution.py:17
  31.0 1.3 collective-permute-start.6
  32.3 4.1 %collective-permute-start.5 = (f32[16,2,1]{2,0,1:T(8,128)S(1)}, f32[16,2,1]{2,0,1:T(8,128)S(1)}, u32[]{:S(2)}, u32[]{:S(2)}) collective-permute-start(f32[16,2,1]{2,0,1:T(8,128)S(1)} %get-tuple-element.167), channel_id=1, source_target_pairs={{0,1},{1,2},{2,3},{4,5},{5,6},{6,7},{8,9},{9,10},{10,11},{12,13},{... | collective-permute-start | bytes 392 | tf_op jit(solution)/shard_map/ppermute | solution.py:17
  37.7 1.3 collective-permute-start.8
  39.0 4.9 %collective-permute-start.7 = (f32[16,2,1]{2,0,1:T(8,128)S(1)}, f32[16,2,1]{2,0,1:T(8,128)S(1)}, u32[]{:S(2)}, u32[]{:S(2)}) collective-permute-start(f32[16,2,1]{2,0,1:T(8,128)S(1)} %get-tuple-element.165), channel_id=1, source_target_pairs={{0,1},{1,2},{2,3},{4,5},{5,6},{6,7},{8,9},{9,10},{10,11},{12,13},{... | collective-permute-start | bytes 392 | tf_op jit(solution)/shard_map/ppermute | solution.py:17
  45.1 1.3 collective-permute-start.10
  46.4 4.9 %collective-permute-start.9 = (f32[16,2,1]{2,0,1:T(8,128)S(1)}, f32[16,2,1]{2,0,1:T(8,128)S(1)}, u32[]{:S(2)}, u32[]{:S(2)}) collective-permute-start(f32[16,2,1]{2,0,1:T(8,128)S(1)} %get-tuple-element.163), channel_id=1, source_target_pairs={{0,1},{1,2},{2,3},{4,5},{5,6},{6,7},{8,9},{9,10},{10,11},{12,13},{... | collective-permute-start | bytes 392 | tf_op jit(solution)/shard_map/ppermute | solution.py:17
  52.5 1.3 collective-permute-start.12
  53.8 4.9 %collective-permute-start.11 = (f32[16,2,1]{2,0,1:T(8,128)S(1)}, f32[16,2,1]{2,0,1:T(8,128)S(1)}, u32[]{:S(2)}, u32[]{:S(2)}) collective-permute-start(f32[16,2,1]{2,0,1:T(8,128)S(1)} %get-tuple-element.161), channel_id=1, source_target_pairs={{0,1},{1,2},{2,3},{4,5},{5,6},{6,7},{8,9},{9,10},{10,11},{12,13},{... | collective-permute-start | bytes 392 | tf_op jit(solution)/shard_map/ppermute | solution.py:17
  59.9 1.3 collective-permute-start.14
  61.2 4.9 %collective-permute-start.13 = (f32[16,2,1]{2,0,1:T(8,128)S(1)}, f32[16,2,1]{2,0,1:T(8,128)S(1)}, u32[]{:S(2)}, u32[]{:S(2)}) collective-permute-start(f32[16,2,1]{2,0,1:T(8,128)S(1)} %get-tuple-element.159), channel_id=1, source_target_pairs={{0,1},{1,2},{2,3},{4,5},{5,6},{6,7},{8,9},{9,10},{10,11},{12,13},{... | collective-permute-start | bytes 392 | tf_op jit(solution)/shard_map/ppermute | solution.py:17
  67.3 1.3 collective-permute-start.16
  68.6 4.9 %collective-permute-start.15 = (f32[16,2,1]{2,0,1:T(8,128)S(1)}, f32[16,2,1]{2,0,1:T(8,128)S(1)}, u32[]{:S(2)}, u32[]{:S(2)}) collective-permute-start(f32[16,2,1]{2,0,1:T(8,128)S(1)} %get-tuple-element.157), channel_id=1, source_target_pairs={{0,1},{1,2},{2,3},{4,5},{5,6},{6,7},{8,9},{9,10},{10,11},{12,13},{... | collective-permute-start | bytes 392 | tf_op jit(solution)/shard_map/ppermute | solution.py:17
  74.7 1.3 collective-permute-start.18
  76.0 4.9 %collective-permute-start.17 = (f32[16,2,1]{2,0,1:T(8,128)S(1)}, f32[16,2,1]{2,0,1:T(8,128)S(1)}, u32[]{:S(2)}, u32[]{:S(2)}) collective-permute-start(f32[16,2,1]{2,0,1:T(8,128)S(1)} %get-tuple-element.155), channel_id=1, source_target_pairs={{0,1},{1,2},{2,3},{4,5},{5,6},{6,7},{8,9},{9,10},{10,11},{12,13},{... | collective-permute-start | bytes 392 | tf_op jit(solution)/shard_map/ppermute | solution.py:17
  82.1 1.3 collective-permute-start.20
  83.4 4.9 %collective-permute-start.19 = (f32[16,2,1]{2,0,1:T(8,128)S(1)}, f32[16,2,1]{2,0,1:T(8,128)S(1)}, u32[]{:S(2)}, u32[]{:S(2)}) collective-permute-start(f32[16,2,1]{2,0,1:T(8,128)S(1)} %get-tuple-element.153), channel_id=1, source_target_pairs={{0,1},{1,2},{2,3},{4,5},{5,6},{6,7},{8,9},{9,10},{10,11},{12,13},{... | collective-permute-start | bytes 392 | tf_op jit(solution)/shard_map/ppermute | solution.py:17
  89.5 1.3 collective-permute-start.22
  90.8 4.9 %collective-permute-start.21 = (f32[16,2,1]{2,0,1:T(8,128)S(1)}, f32[16,2,1]{2,0,1:T(8,128)S(1)}, u32[]{:S(2)}, u32[]{:S(2)}) collective-permute-start(f32[16,2,1]{2,0,1:T(8,128)S(1)} %get-tuple-element.151), channel_id=1, source_target_pairs={{0,1},{1,2},{2,3},{4,5},{5,6},{6,7},{8,9},{9,10},{10,11},{12,13},{... | collective-permute-start | bytes 392 | tf_op jit(solution)/shard_map/ppermute | solution.py:17
  96.9 1.3 collective-permute-start.24
  98.2 4.9 %collective-permute-start.23 = (f32[16,2,1]{2,0,1:T(8,128)S(1)}, f32[16,2,1]{2,0,1:T(8,128)S(1)}, u32[]{:S(2)}, u32[]{:S(2)}) collective-permute-start(f32[16,2,1]{2,0,1:T(8,128)S(1)} %get-tuple-element.149), channel_id=1, source_target_pairs={{0,1},{1,2},{2,3},{4,5},{5,6},{6,7},{8,9},{9,10},{10,11},{12,13},{... | collective-permute-start | bytes 392 | tf_op jit(solution)/shard_map/ppermute | solution.py:17
  104.3 1.3 collective-permute-start.26
  105.6 4.9 %collective-permute-start.25 = (f32[16,2,1]{2,0,1:T(8,128)S(1)}, f32[16,2,1]{2,0,1:T(8,128)S(1)}, u32[]{:S(2)}, u32[]{:S(2)}) collective-permute-start(f32[16,2,1]{2,0,1:T(8,128)S(1)} %get-tuple-element.147), channel_id=1, source_target_pairs={{0,1},{1,2},{2,3},{4,5},{5,6},{6,7},{8,9},{9,10},{10,11},{12,13},{... | collective-permute-start | bytes 392 | tf_op jit(solution)/shard_map/ppermute | solution.py:17
  113.0 5.0 %collective-permute-start.27 = (f32[16,2,1]{2,0,1:T(8,128)S(1)}, f32[16,2,1]{2,0,1:T(8,128)S(1)}, u32[]{:S(2)}, u32[]{:S(2)}) collective-permute-start(f32[16,2,1]{2,0,1:T(8,128)S(1)} %get-tuple-element.145), channel_id=1, source_target_pairs={{0,1},{1,2},{2,3},{4,5},{5,6},{6,7},{8,9},{9,10},{10,11},{12,13},{... | collective-permute-start | bytes 392 | tf_op jit(solution)/shard_map/ppermute | solution.py:17
  120.4 4.9 %collective-permute-start.29 = (f32[16,2,1]{2,0,1:T(8,128)S(1)}, f32[16,2,1]{2,0,1:T(8,128)S(1)}, u32[]{:S(2)}, u32[]{:S(2)}) collective-permute-start(f32[16,2,1]{2,0,1:T(8,128)S(1)} %get-tuple-element.143), channel_id=1, source_target_pairs={{0,1},{1,2},{2,3},{4,5},{5,6},{6,7},{8,9},{9,10},{10,11},{12,13},{... | collective-permute-start | bytes 392 | tf_op jit(solution)/shard_map/ppermute | solution.py:17
  126.5 1.4 collective-permute-start.32
  127.9 4.9 %collective-permute-start.31 = (f32[16,2,1]{2,0,1:T(8,128)S(1)}, f32[16,2,1]{2,0,1:T(8,128)S(1)}, u32[]{:S(2)}, u32[]{:S(2)}) collective-permute-start(f32[16,2,1]{2,0,1:T(8,128)S(1)} %get-tuple-element.141), channel_id=1, source_target_pairs={{0,1},{1,2},{2,3},{4,5},{5,6},{6,7},{8,9},{9,10},{10,11},{12,13},{... | collective-permute-start | bytes 392 | tf_op jit(solution)/shard_map/ppermute | solution.py:17
  134.6 1.6 maximum_reduce_fusion
  136.4 7.9 %multiply_subtract_fusion = (f32[16,2,512]{2,0,1:T(8,128)S(1)}, f32[16,2,512]{2,0,1:T(8,128)S(1)}) fusion(f32[16,2,512]{2,0,1:T(8,128)S(1)} %copy.39, bf16[2,512,2,2048]{3,2,1,0:T(2,128)(2,1)} %param.9, bf16[16,2,2048]{2,0,1:T(8,128)(2,1)S(1)} %all_gather.6), kind=kOutput, calls=%fused_computation.216 | convolution fusion | flops 134266880 | bytes 8716288 | tf_op jit(solution)/shard_map/fiqj,bqj->bfi/dot_general | solution.py:38
  144.3 128.0 %while.10 = (s32[]{:T(128)}, f32[16,2,512]{2,0,1:T(8,128)S(1)}, pred[]{:T(512)}, f32[1,2,512]{2,1,0:T(2,128)S(1)}, bf16[2,512,2,2048]{3,1,2,0:T(8,128)(2,1)}, /*index=5*/f32[16,2,512]{2,0,1:T(8,128)S(1)}, s32[]{:T(128)}) while((s32[]{:T(128)}, f32[16,2,512]{2,0,1:T(8,128)S(1)}, pred[]{:T(512)}, f32[1,2,512]{2,1,0:T(2,128)S(1)}, ...), condition=%wide.region_3.4_spmd, body=%wide.region_2.3_spmd.sunk | while | flops 134283264 | bytes 9244790 | solution.py:71
  144.3 1.3 collective-permute-start
  145.6 4.9 %collective-permute-done = f32[16,2,512]{2,0,1:T(8,128)S(1)} collective-permute-done((f32[16,2,512]{2,0,1:T(8,128)S(1)}, f32[16,2,512]{2,0,1:T(8,128)S(1)}, u32[]{:S(2)}, u32[]{:S(2)}) %collective-permute-start) | collective-permute-done | bytes 65568 | tf_op jit(solution)/shard_map/while/body/eval_jaxpr/ppermute | solution.py:26
  150.5 8.0 %all_gather.8 = bf16[16,2,2048]{2,0,1:T(8,128)(2,1)S(1)} all-gather(bf16[16,2,512]{2,0,1:T(8,128)(2,1)S(1)} %multiply_convert_fusion.2), channel_id=1, replica_groups=mesh['cuts'=8,'space'=4] {'space'}, dimensions={2}, use_global_device_ids=true | all-gather | bytes 163840 | tf_op jit(solution)/shard_map/while/body/eval_jaxpr/all_gather | solution.py:68
  158.5 5.7 %fusion.76 = f32[16,2,512]{2,0,1:T(8,128)S(1)} fusion(f32[16,2,512]{2,0,1:T(8,128)S(1)} %get-tuple-element.217, f32[16,2,512]{2,0,1:T(8,128)S(1)} %get-tuple-element.228, bf16[2,512,2,2048]{3,1,2,0:T(8,128)(2,1)} %get-tuple-element.227, bf16[16,2,2048]{2,0,1:T(8,128)(2,1)S(1)} %all_gather.8, pred[]{:T(512)} %get-tuple-element.225), kind=kOutput, calls=%fused_computation.2.clone.1 | convolution fusion | flops 134250496 | bytes 8716289 | tf_op jit(solution)/shard_map/while/body/eval_jaxpr/fiqj,bqj->bfi/dot_general | solution.py:38
  164.2 1.3 collective-permute-start
  165.5 4.9 %collective-permute-done = f32[16,2,512]{2,0,1:T(8,128)S(1)} collective-permute-done((f32[16,2,512]{2,0,1:T(8,128)S(1)}, f32[16,2,512]{2,0,1:T(8,128)S(1)}, u32[]{:S(2)}, u32[]{:S(2)}) %collective-permute-start) | collective-permute-done | bytes 65568 | tf_op jit(solution)/shard_map/while/body/eval_jaxpr/ppermute | solution.py:26
  170.4 5.4 %all_gather.8 = bf16[16,2,2048]{2,0,1:T(8,128)(2,1)S(1)} all-gather(bf16[16,2,512]{2,0,1:T(8,128)(2,1)S(1)} %multiply_convert_fusion.2), channel_id=1, replica_groups=mesh['cuts'=8,'space'=4] {'space'}, dimensions={2}, use_global_device_ids=true | all-gather | bytes 163840 | tf_op jit(solution)/shard_map/while/body/eval_jaxpr/all_gather | solution.py:68
  175.8 5.7 %fusion.76 = f32[16,2,512]{2,0,1:T(8,128)S(1)} fusion(f32[16,2,512]{2,0,1:T(8,128)S(1)} %get-tuple-element.217, f32[16,2,512]{2,0,1:T(8,128)S(1)} %get-tuple-element.228, bf16[2,512,2,2048]{3,1,2,0:T(8,128)(2,1)} %get-tuple-element.227, bf16[16,2,2048]{2,0,1:T(8,128)(2,1)S(1)} %all_gather.8, pred[]{:T(512)} %get-tuple-element.225), kind=kOutput, calls=%fused_computation.2.clone.1 | convolution fusion | flops 134250496 | bytes 8716289 | tf_op jit(solution)/shard_map/while/body/eval_jaxpr/fiqj,bqj->bfi/dot_general | solution.py:38
  181.5 1.3 collective-permute-start
  182.8 5.5 %collective-permute-done = f32[16,2,512]{2,0,1:T(8,128)S(1)} collective-permute-done((f32[16,2,512]{2,0,1:T(8,128)S(1)}, f32[16,2,512]{2,0,1:T(8,128)S(1)}, u32[]{:S(2)}, u32[]{:S(2)}) %collective-permute-start) | collective-permute-done | bytes 65568 | tf_op jit(solution)/shard_map/while/body/eval_jaxpr/ppermute | solution.py:26
  188.3 5.4 %all_gather.8 = bf16[16,2,2048]{2,0,1:T(8,128)(2,1)S(1)} all-gather(bf16[16,2,512]{2,0,1:T(8,128)(2,1)S(1)} %multiply_convert_fusion.2), channel_id=1, replica_groups=mesh['cuts'=8,'space'=4] {'space'}, dimensions={2}, use_global_device_ids=true | all-gather | bytes 163840 | tf_op jit(solution)/shard_map/while/body/eval_jaxpr/all_gather | solution.py:68
  193.8 5.7 %fusion.76 = f32[16,2,512]{2,0,1:T(8,128)S(1)} fusion(f32[16,2,512]{2,0,1:T(8,128)S(1)} %get-tuple-element.217, f32[16,2,512]{2,0,1:T(8,128)S(1)} %get-tuple-element.228, bf16[2,512,2,2048]{3,1,2,0:T(8,128)(2,1)} %get-tuple-element.227, bf16[16,2,2048]{2,0,1:T(8,128)(2,1)S(1)} %all_gather.8, pred[]{:T(512)} %get-tuple-element.225), kind=kOutput, calls=%fused_computation.2.clone.1 | convolution fusion | flops 134250496 | bytes 8716289 | tf_op jit(solution)/shard_map/while/body/eval_jaxpr/fiqj,bqj->bfi/dot_general | solution.py:38
  199.4 1.3 collective-permute-start
  200.7 5.8 %collective-permute-done = f32[16,2,512]{2,0,1:T(8,128)S(1)} collective-permute-done((f32[16,2,512]{2,0,1:T(8,128)S(1)}, f32[16,2,512]{2,0,1:T(8,128)S(1)}, u32[]{:S(2)}, u32[]{:S(2)}) %collective-permute-start) | collective-permute-done | bytes 65568 | tf_op jit(solution)/shard_map/while/body/eval_jaxpr/ppermute | solution.py:26
  206.6 5.4 %all_gather.8 = bf16[16,2,2048]{2,0,1:T(8,128)(2,1)S(1)} all-gather(bf16[16,2,512]{2,0,1:T(8,128)(2,1)S(1)} %multiply_convert_fusion.2), channel_id=1, replica_groups=mesh['cuts'=8,'space'=4] {'space'}, dimensions={2}, use_global_device_ids=true | all-gather | bytes 163840 | tf_op jit(solution)/shard_map/while/body/eval_jaxpr/all_gather | solution.py:68
  212.0 5.7 %fusion.76 = f32[16,2,512]{2,0,1:T(8,128)S(1)} fusion(f32[16,2,512]{2,0,1:T(8,128)S(1)} %get-tuple-element.217, f32[16,2,512]{2,0,1:T(8,128)S(1)} %get-tuple-element.228, bf16[2,512,2,2048]{3,1,2,0:T(8,128)(2,1)} %get-tuple-element.227, bf16[16,2,2048]{2,0,1:T(8,128)(2,1)S(1)} %all_gather.8, pred[]{:T(512)} %get-tuple-element.225), kind=kOutput, calls=%fused_computation.2.clone.1 | convolution fusion | flops 134250496 | bytes 8716289 | tf_op jit(solution)/shard_map/while/body/eval_jaxpr/fiqj,bqj->bfi/dot_general | solution.py:38
  217.6 1.3 collective-permute-start
  218.9 5.8 %collective-permute-done = f32[16,2,512]{2,0,1:T(8,128)S(1)} collective-permute-done((f32[16,2,512]{2,0,1:T(8,128)S(1)}, f32[16,2,512]{2,0,1:T(8,128)S(1)}, u32[]{:S(2)}, u32[]{:S(2)}) %collective-permute-start) | collective-permute-done | bytes 65568 | tf_op jit(solution)/shard_map/while/body/eval_jaxpr/ppermute | solution.py:26
  224.8 5.4 %all_gather.8 = bf16[16,2,2048]{2,0,1:T(8,128)(2,1)S(1)} all-gather(bf16[16,2,512]{2,0,1:T(8,128)(2,1)S(1)} %multiply_convert_fusion.2), channel_id=1, replica_groups=mesh['cuts'=8,'space'=4] {'space'}, dimensions={2}, use_global_device_ids=true | all-gather | bytes 163840 | tf_op jit(solution)/shard_map/while/body/eval_jaxpr/all_gather | solution.py:68
  230.2 5.7 %fusion.76 = f32[16,2,512]{2,0,1:T(8,128)S(1)} fusion(f32[16,2,512]{2,0,1:T(8,128)S(1)} %get-tuple-element.217, f32[16,2,512]{2,0,1:T(8,128)S(1)} %get-tuple-element.228, bf16[2,512,2,2048]{3,1,2,0:T(8,128)(2,1)} %get-tuple-element.227, bf16[16,2,2048]{2,0,1:T(8,128)(2,1)S(1)} %all_gather.8, pred[]{:T(512)} %get-tuple-element.225), kind=kOutput, calls=%fused_computation.2.clone.1 | convolution fusion | flops 134250496 | bytes 8716289 | tf_op jit(solution)/shard_map/while/body/eval_jaxpr/fiqj,bqj->bfi/dot_general | solution.py:38
  235.8 1.3 collective-permute-start
  237.1 5.8 %collective-permute-done = f32[16,2,512]{2,0,1:T(8,128)S(1)} collective-permute-done((f32[16,2,512]{2,0,1:T(8,128)S(1)}, f32[16,2,512]{2,0,1:T(8,128)S(1)}, u32[]{:S(2)}, u32[]{:S(2)}) %collective-permute-start) | collective-permute-done | bytes 65568 | tf_op jit(solution)/shard_map/while/body/eval_jaxpr/ppermute | solution.py:26
  243.0 5.4 %all_gather.8 = bf16[16,2,2048]{2,0,1:T(8,128)(2,1)S(1)} all-gather(bf16[16,2,512]{2,0,1:T(8,128)(2,1)S(1)} %multiply_convert_fusion.2), channel_id=1, replica_groups=mesh['cuts'=8,'space'=4] {'space'}, dimensions={2}, use_global_device_ids=true | all-gather | bytes 163840 | tf_op jit(solution)/shard_map/while/body/eval_jaxpr/all_gather | solution.py:68
  248.4 5.7 %fusion.76 = f32[16,2,512]{2,0,1:T(8,128)S(1)} fusion(f32[16,2,512]{2,0,1:T(8,128)S(1)} %get-tuple-element.217, f32[16,2,512]{2,0,1:T(8,128)S(1)} %get-tuple-element.228, bf16[2,512,2,2048]{3,1,2,0:T(8,128)(2,1)} %get-tuple-element.227, bf16[16,2,2048]{2,0,1:T(8,128)(2,1)S(1)} %all_gather.8, pred[]{:T(512)} %get-tuple-element.225), kind=kOutput, calls=%fused_computation.2.clone.1 | convolution fusion | flops 134250496 | bytes 8716289 | tf_op jit(solution)/shard_map/while/body/eval_jaxpr/fiqj,bqj->bfi/dot_general | solution.py:38
  254.1 1.3 collective-permute-start
  255.4 5.8 %collective-permute-done = f32[16,2,512]{2,0,1:T(8,128)S(1)} collective-permute-done((f32[16,2,512]{2,0,1:T(8,128)S(1)}, f32[16,2,512]{2,0,1:T(8,128)S(1)}, u32[]{:S(2)}, u32[]{:S(2)}) %collective-permute-start) | collective-permute-done | bytes 65568 | tf_op jit(solution)/shard_map/while/body/eval_jaxpr/ppermute | solution.py:26
  261.2 5.4 %all_gather.8 = bf16[16,2,2048]{2,0,1:T(8,128)(2,1)S(1)} all-gather(bf16[16,2,512]{2,0,1:T(8,128)(2,1)S(1)} %multiply_convert_fusion.2), channel_id=1, replica_groups=mesh['cuts'=8,'space'=4] {'space'}, dimensions={2}, use_global_device_ids=true | all-gather | bytes 163840 | tf_op jit(solution)/shard_map/while/body/eval_jaxpr/all_gather | solution.py:68
  266.6 5.7 %fusion.76 = f32[16,2,512]{2,0,1:T(8,128)S(1)} fusion(f32[16,2,512]{2,0,1:T(8,128)S(1)} %get-tuple-element.217, f32[16,2,512]{2,0,1:T(8,128)S(1)} %get-tuple-element.228, bf16[2,512,2,2048]{3,1,2,0:T(8,128)(2,1)} %get-tuple-element.227, bf16[16,2,2048]{2,0,1:T(8,128)(2,1)S(1)} %all_gather.8, pred[]{:T(512)} %get-tuple-element.225), kind=kOutput, calls=%fused_computation.2.clone.1 | convolution fusion | flops 134250496 | bytes 8716289 | tf_op jit(solution)/shard_map/while/body/eval_jaxpr/fiqj,bqj->bfi/dot_general | solution.py:38
  (132 shorter events, 25.4 us)
Async XLA Ops:
  1.4 23.5 %collective-permute-start.2 = (f32[16,2,1]{0,2,1:T(1,128)S(1)}, f32[16,2,1]{0,2,1:T(1,128)S(1)}, u32[]{:S(2)}, u32[]{:S(2)}) collective-permute-start(f32[16,2,1]{0,2,1:T(1,128)S(1)} %get-tuple-element.74), channel_id=1, source_target_pairs={{1,0},{2,1},{3,2},{5,4},{6,5},{7,6},{9,8},{10,9},{11,10},{13,12},{... | collective-permute-start | bytes 392 | tf_op jit(solution)/shard_map/ppermute | solution.py:18
  2.7 22.1 %collective-permute-start.1 = (f32[16,2,1]{0,2,1:T(1,128)S(1)}, f32[16,2,1]{0,2,1:T(1,128)S(1)}, u32[]{:S(2)}, u32[]{:S(2)}) collective-permute-start(f32[16,2,1]{0,2,1:T(1,128)S(1)} %get-tuple-element.75), channel_id=1, source_target_pairs={{0,1},{1,2},{2,3},{4,5},{5,6},{6,7},{8,9},{9,10},{10,11},{12,13},{... | collective-permute-start | bytes 392 | tf_op jit(solution)/shard_map/ppermute | solution.py:17
  25.4 4.4 %collective-permute-start.4 = (f32[16,2,1]{2,0,1:T(8,128)S(1)}, f32[16,2,1]{2,0,1:T(8,128)S(1)}, u32[]{:S(2)}, u32[]{:S(2)}) collective-permute-start(f32[16,2,1]{2,0,1:T(8,128)S(1)} %get-tuple-element.168), channel_id=1, source_target_pairs={{1,0},{2,1},{3,2},{5,4},{6,5},{7,6},{9,8},{10,9},{11,10},{13,12},{... | collective-permute-start | bytes 392 | tf_op jit(solution)/shard_map/ppermute | solution.py:18
  26.7 3.9 %collective-permute-start.3 = (f32[16,2,1]{2,0,1:T(8,128)S(1)}, f32[16,2,1]{2,0,1:T(8,128)S(1)}, u32[]{:S(2)}, u32[]{:S(2)}) collective-permute-start(f32[16,2,1]{2,0,1:T(8,128)S(1)} %get-tuple-element.169), channel_id=1, source_target_pairs={{0,1},{1,2},{2,3},{4,5},{5,6},{6,7},{8,9},{9,10},{10,11},{12,13},{... | collective-permute-start | bytes 392 | tf_op jit(solution)/shard_map/ppermute | solution.py:17
  31.0 5.5 %collective-permute-start.6 = (f32[16,2,1]{2,0,1:T(8,128)S(1)}, f32[16,2,1]{2,0,1:T(8,128)S(1)}, u32[]{:S(2)}, u32[]{:S(2)}) collective-permute-start(f32[16,2,1]{2,0,1:T(8,128)S(1)} %get-tuple-element.166), channel_id=1, source_target_pairs={{1,0},{2,1},{3,2},{5,4},{6,5},{7,6},{9,8},{10,9},{11,10},{13,12},{... | collective-permute-start | bytes 392 | tf_op jit(solution)/shard_map/ppermute | solution.py:18
  32.3 5.0 %collective-permute-start.5 = (f32[16,2,1]{2,0,1:T(8,128)S(1)}, f32[16,2,1]{2,0,1:T(8,128)S(1)}, u32[]{:S(2)}, u32[]{:S(2)}) collective-permute-start(f32[16,2,1]{2,0,1:T(8,128)S(1)} %get-tuple-element.167), channel_id=1, source_target_pairs={{0,1},{1,2},{2,3},{4,5},{5,6},{6,7},{8,9},{9,10},{10,11},{12,13},{... | collective-permute-start | bytes 392 | tf_op jit(solution)/shard_map/ppermute | solution.py:17
  37.7 6.2 %collective-permute-start.8 = (f32[16,2,1]{2,0,1:T(8,128)S(1)}, f32[16,2,1]{2,0,1:T(8,128)S(1)}, u32[]{:S(2)}, u32[]{:S(2)}) collective-permute-start(f32[16,2,1]{2,0,1:T(8,128)S(1)} %get-tuple-element.164), channel_id=1, source_target_pairs={{1,0},{2,1},{3,2},{5,4},{6,5},{7,6},{9,8},{10,9},{11,10},{13,12},{... | collective-permute-start | bytes 392 | tf_op jit(solution)/shard_map/ppermute | solution.py:18
  39.0 5.7 %collective-permute-start.7 = (f32[16,2,1]{2,0,1:T(8,128)S(1)}, f32[16,2,1]{2,0,1:T(8,128)S(1)}, u32[]{:S(2)}, u32[]{:S(2)}) collective-permute-start(f32[16,2,1]{2,0,1:T(8,128)S(1)} %get-tuple-element.165), channel_id=1, source_target_pairs={{0,1},{1,2},{2,3},{4,5},{5,6},{6,7},{8,9},{9,10},{10,11},{12,13},{... | collective-permute-start | bytes 392 | tf_op jit(solution)/shard_map/ppermute | solution.py:17
  45.1 6.2 %collective-permute-start.10 = (f32[16,2,1]{2,0,1:T(8,128)S(1)}, f32[16,2,1]{2,0,1:T(8,128)S(1)}, u32[]{:S(2)}, u32[]{:S(2)}) collective-permute-start(f32[16,2,1]{2,0,1:T(8,128)S(1)} %get-tuple-element.162), channel_id=1, source_target_pairs={{1,0},{2,1},{3,2},{5,4},{6,5},{7,6},{9,8},{10,9},{11,10},{13,12},{... | collective-permute-start | bytes 392 | tf_op jit(solution)/shard_map/ppermute | solution.py:18
  46.4 5.7 %collective-permute-start.9 = (f32[16,2,1]{2,0,1:T(8,128)S(1)}, f32[16,2,1]{2,0,1:T(8,128)S(1)}, u32[]{:S(2)}, u32[]{:S(2)}) collective-permute-start(f32[16,2,1]{2,0,1:T(8,128)S(1)} %get-tuple-element.163), channel_id=1, source_target_pairs={{0,1},{1,2},{2,3},{4,5},{5,6},{6,7},{8,9},{9,10},{10,11},{12,13},{... | collective-permute-start | bytes 392 | tf_op jit(solution)/shard_map/ppermute | solution.py:17
  52.5 6.2 %collective-permute-start.12 = (f32[16,2,1]{2,0,1:T(8,128)S(1)}, f32[16,2,1]{2,0,1:T(8,128)S(1)}, u32[]{:S(2)}, u32[]{:S(2)}) collective-permute-start(f32[16,2,1]{2,0,1:T(8,128)S(1)} %get-tuple-element.160), channel_id=1, source_target_pairs={{1,0},{2,1},{3,2},{5,4},{6,5},{7,6},{9,8},{10,9},{11,10},{13,12},{... | collective-permute-start | bytes 392 | tf_op jit(solution)/shard_map/ppermute | solution.py:18
  53.8 5.7 %collective-permute-start.11 = (f32[16,2,1]{2,0,1:T(8,128)S(1)}, f32[16,2,1]{2,0,1:T(8,128)S(1)}, u32[]{:S(2)}, u32[]{:S(2)}) collective-permute-start(f32[16,2,1]{2,0,1:T(8,128)S(1)} %get-tuple-element.161), channel_id=1, source_target_pairs={{0,1},{1,2},{2,3},{4,5},{5,6},{6,7},{8,9},{9,10},{10,11},{12,13},{... | collective-permute-start | bytes 392 | tf_op jit(solution)/shard_map/ppermute | solution.py:17
  59.9 6.2 %collective-permute-start.14 = (f32[16,2,1]{2,0,1:T(8,128)S(1)}, f32[16,2,1]{2,0,1:T(8,128)S(1)}, u32[]{:S(2)}, u32[]{:S(2)}) collective-permute-start(f32[16,2,1]{2,0,1:T(8,128)S(1)} %get-tuple-element.158), channel_id=1, source_target_pairs={{1,0},{2,1},{3,2},{5,4},{6,5},{7,6},{9,8},{10,9},{11,10},{13,12},{... | collective-permute-start | bytes 392 | tf_op jit(solution)/shard_map/ppermute | solution.py:18
  61.2 5.7 %collective-permute-start.13 = (f32[16,2,1]{2,0,1:T(8,128)S(1)}, f32[16,2,1]{2,0,1:T(8,128)S(1)}, u32[]{:S(2)}, u32[]{:S(2)}) collective-permute-start(f32[16,2,1]{2,0,1:T(8,128)S(1)} %get-tuple-element.159), channel_id=1, source_target_pairs={{0,1},{1,2},{2,3},{4,5},{5,6},{6,7},{8,9},{9,10},{10,11},{12,13},{... | collective-permute-start | bytes 392 | tf_op jit(solution)/shard_map/ppermute | solution.py:17
  67.3 6.2 %collective-permute-start.16 = (f32[16,2,1]{2,0,1:T(8,128)S(1)}, f32[16,2,1]{2,0,1:T(8,128)S(1)}, u32[]{:S(2)}, u32[]{:S(2)}) collective-permute-start(f32[16,2,1]{2,0,1:T(8,128)S(1)} %get-tuple-element.156), channel_id=1, source_target_pairs={{1,0},{2,1},{3,2},{5,4},{6,5},{7,6},{9,8},{10,9},{11,10},{13,12},{... | collective-permute-start | bytes 392 | tf_op jit(solution)/shard_map/ppermute | solution.py:18
  68.6 5.7 %collective-permute-start.15 = (f32[16,2,1]{2,0,1:T(8,128)S(1)}, f32[16,2,1]{2,0,1:T(8,128)S(1)}, u32[]{:S(2)}, u32[]{:S(2)}) collective-permute-start(f32[16,2,1]{2,0,1:T(8,128)S(1)} %get-tuple-element.157), channel_id=1, source_target_pairs={{0,1},{1,2},{2,3},{4,5},{5,6},{6,7},{8,9},{9,10},{10,11},{12,13},{... | collective-permute-start | bytes 392 | tf_op jit(solution)/shard_map/ppermute | solution.py:17
  74.7 6.2 %collective-permute-start.18 = (f32[16,2,1]{2,0,1:T(8,128)S(1)}, f32[16,2,1]{2,0,1:T(8,128)S(1)}, u32[]{:S(2)}, u32[]{:S(2)}) collective-permute-start(f32[16,2,1]{2,0,1:T(8,128)S(1)} %get-tuple-element.154), channel_id=1, source_target_pairs={{1,0},{2,1},{3,2},{5,4},{6,5},{7,6},{9,8},{10,9},{11,10},{13,12},{... | collective-permute-start | bytes 392 | tf_op jit(solution)/shard_map/ppermute | solution.py:18
  76.0 5.7 %collective-permute-start.17 = (f32[16,2,1]{2,0,1:T(8,128)S(1)}, f32[16,2,1]{2,0,1:T(8,128)S(1)}, u32[]{:S(2)}, u32[]{:S(2)}) collective-permute-start(f32[16,2,1]{2,0,1:T(8,128)S(1)} %get-tuple-element.155), channel_id=1, source_target_pairs={{0,1},{1,2},{2,3},{4,5},{5,6},{6,7},{8,9},{9,10},{10,11},{12,13},{... | collective-permute-start | bytes 392 | tf_op jit(solution)/shard_map/ppermute | solution.py:17
  82.1 6.2 %collective-permute-start.20 = (f32[16,2,1]{2,0,1:T(8,128)S(1)}, f32[16,2,1]{2,0,1:T(8,128)S(1)}, u32[]{:S(2)}, u32[]{:S(2)}) collective-permute-start(f32[16,2,1]{2,0,1:T(8,128)S(1)} %get-tuple-element.152), channel_id=1, source_target_pairs={{1,0},{2,1},{3,2},{5,4},{6,5},{7,6},{9,8},{10,9},{11,10},{13,12},{... | collective-permute-start | bytes 392 | tf_op jit(solution)/shard_map/ppermute | solution.py:18
  83.4 5.7 %collective-permute-start.19 = (f32[16,2,1]{2,0,1:T(8,128)S(1)}, f32[16,2,1]{2,0,1:T(8,128)S(1)}, u32[]{:S(2)}, u32[]{:S(2)}) collective-permute-start(f32[16,2,1]{2,0,1:T(8,128)S(1)} %get-tuple-element.153), channel_id=1, source_target_pairs={{0,1},{1,2},{2,3},{4,5},{5,6},{6,7},{8,9},{9,10},{10,11},{12,13},{... | collective-permute-start | bytes 392 | tf_op jit(solution)/shard_map/ppermute | solution.py:17
  89.5 6.2 %collective-permute-start.22 = (f32[16,2,1]{2,0,1:T(8,128)S(1)}, f32[16,2,1]{2,0,1:T(8,128)S(1)}, u32[]{:S(2)}, u32[]{:S(2)}) collective-permute-start(f32[16,2,1]{2,0,1:T(8,128)S(1)} %get-tuple-element.150), channel_id=1, source_target_pairs={{1,0},{2,1},{3,2},{5,4},{6,5},{7,6},{9,8},{10,9},{11,10},{13,12},{... | collective-permute-start | bytes 392 | tf_op jit(solution)/shard_map/ppermute | solution.py:18
  90.8 5.7 %collective-permute-start.21 = (f32[16,2,1]{2,0,1:T(8,128)S(1)}, f32[16,2,1]{2,0,1:T(8,128)S(1)}, u32[]{:S(2)}, u32[]{:S(2)}) collective-permute-start(f32[16,2,1]{2,0,1:T(8,128)S(1)} %get-tuple-element.151), channel_id=1, source_target_pairs={{0,1},{1,2},{2,3},{4,5},{5,6},{6,7},{8,9},{9,10},{10,11},{12,13},{... | collective-permute-start | bytes 392 | tf_op jit(solution)/shard_map/ppermute | solution.py:17
  96.9 6.2 %collective-permute-start.24 = (f32[16,2,1]{2,0,1:T(8,128)S(1)}, f32[16,2,1]{2,0,1:T(8,128)S(1)}, u32[]{:S(2)}, u32[]{:S(2)}) collective-permute-start(f32[16,2,1]{2,0,1:T(8,128)S(1)} %get-tuple-element.148), channel_id=1, source_target_pairs={{1,0},{2,1},{3,2},{5,4},{6,5},{7,6},{9,8},{10,9},{11,10},{13,12},{... | collective-permute-start | bytes 392 | tf_op jit(solution)/shard_map/ppermute | solution.py:18
  98.2 5.7 %collective-permute-start.23 = (f32[16,2,1]{2,0,1:T(8,128)S(1)}, f32[16,2,1]{2,0,1:T(8,128)S(1)}, u32[]{:S(2)}, u32[]{:S(2)}) collective-permute-start(f32[16,2,1]{2,0,1:T(8,128)S(1)} %get-tuple-element.149), channel_id=1, source_target_pairs={{0,1},{1,2},{2,3},{4,5},{5,6},{6,7},{8,9},{9,10},{10,11},{12,13},{... | collective-permute-start | bytes 392 | tf_op jit(solution)/shard_map/ppermute | solution.py:17
  104.3 6.2 %collective-permute-start.26 = (f32[16,2,1]{2,0,1:T(8,128)S(1)}, f32[16,2,1]{2,0,1:T(8,128)S(1)}, u32[]{:S(2)}, u32[]{:S(2)}) collective-permute-start(f32[16,2,1]{2,0,1:T(8,128)S(1)} %get-tuple-element.146), channel_id=1, source_target_pairs={{1,0},{2,1},{3,2},{5,4},{6,5},{7,6},{9,8},{10,9},{11,10},{13,12},{... | collective-permute-start | bytes 392 | tf_op jit(solution)/shard_map/ppermute | solution.py:18
  105.6 5.7 %collective-permute-start.25 = (f32[16,2,1]{2,0,1:T(8,128)S(1)}, f32[16,2,1]{2,0,1:T(8,128)S(1)}, u32[]{:S(2)}, u32[]{:S(2)}) collective-permute-start(f32[16,2,1]{2,0,1:T(8,128)S(1)} %get-tuple-element.147), channel_id=1, source_target_pairs={{0,1},{1,2},{2,3},{4,5},{5,6},{6,7},{8,9},{9,10},{10,11},{12,13},{... | collective-permute-start | bytes 392 | tf_op jit(solution)/shard_map/ppermute | solution.py:17
  111.7 6.4 %collective-permute-start.28 = (f32[16,2,1]{2,0,1:T(8,128)S(1)}, f32[16,2,1]{2,0,1:T(8,128)S(1)}, u32[]{:S(2)}, u32[]{:S(2)}) collective-permute-start(f32[16,2,1]{2,0,1:T(8,128)S(1)} %get-tuple-element.144), channel_id=1, source_target_pairs={{1,0},{2,1},{3,2},{5,4},{6,5},{7,6},{9,8},{10,9},{11,10},{13,12},{... | collective-permute-start | bytes 392 | tf_op jit(solution)/shard_map/ppermute | solution.py:18
  113.0 5.7 %collective-permute-start.27 = (f32[16,2,1]{2,0,1:T(8,128)S(1)}, f32[16,2,1]{2,0,1:T(8,128)S(1)}, u32[]{:S(2)}, u32[]{:S(2)}) collective-permute-start(f32[16,2,1]{2,0,1:T(8,128)S(1)} %get-tuple-element.145), channel_id=1, source_target_pairs={{0,1},{1,2},{2,3},{4,5},{5,6},{6,7},{8,9},{9,10},{10,11},{12,13},{... | collective-permute-start | bytes 392 | tf_op jit(solution)/shard_map/ppermute | solution.py:17
  119.1 6.2 %collective-permute-start.30 = (f32[16,2,1]{2,0,1:T(8,128)S(1)}, f32[16,2,1]{2,0,1:T(8,128)S(1)}, u32[]{:S(2)}, u32[]{:S(2)}) collective-permute-start(f32[16,2,1]{2,0,1:T(8,128)S(1)} %get-tuple-element.142), channel_id=1, source_target_pairs={{1,0},{2,1},{3,2},{5,4},{6,5},{7,6},{9,8},{10,9},{11,10},{13,12},{... | collective-permute-start | bytes 392 | tf_op jit(solution)/shard_map/ppermute | solution.py:18
  120.4 5.7 %collective-permute-start.29 = (f32[16,2,1]{2,0,1:T(8,128)S(1)}, f32[16,2,1]{2,0,1:T(8,128)S(1)}, u32[]{:S(2)}, u32[]{:S(2)}) collective-permute-start(f32[16,2,1]{2,0,1:T(8,128)S(1)} %get-tuple-element.143), channel_id=1, source_target_pairs={{0,1},{1,2},{2,3},{4,5},{5,6},{6,7},{8,9},{9,10},{10,11},{12,13},{... | collective-permute-start | bytes 392 | tf_op jit(solution)/shard_map/ppermute | solution.py:17
  126.5 17.8 %copy-start = (f32[1,2,512]{2,1,0:T(2,128)S(1)}, f32[1,2,512]{2,1,0:T(2,128)}, u32[]{:S(2)}) copy-start(f32[1,2,512]{2,1,0:T(2,128)} %param.8) | copy-start | bytes 12292
  126.5 6.3 %collective-permute-start.32 = (f32[16,2,1]{2,0,1:T(8,128)S(1)}, f32[16,2,1]{2,0,1:T(8,128)S(1)}, u32[]{:S(2)}, u32[]{:S(2)}) collective-permute-start(f32[16,2,1]{2,0,1:T(8,128)S(1)} %get-tuple-element.140), channel_id=1, source_target_pairs={{1,0},{2,1},{3,2},{5,4},{6,5},{7,6},{9,8},{10,9},{11,10},{13,12},{... | collective-permute-start | bytes 392 | tf_op jit(solution)/shard_map/ppermute | solution.py:18
  127.9 5.7 %collective-permute-start.31 = (f32[16,2,1]{2,0,1:T(8,128)S(1)}, f32[16,2,1]{2,0,1:T(8,128)S(1)}, u32[]{:S(2)}, u32[]{:S(2)}) collective-permute-start(f32[16,2,1]{2,0,1:T(8,128)S(1)} %get-tuple-element.141), channel_id=1, source_target_pairs={{0,1},{1,2},{2,3},{4,5},{5,6},{6,7},{8,9},{9,10},{10,11},{12,13},{... | collective-permute-start | bytes 392 | tf_op jit(solution)/shard_map/ppermute | solution.py:17
  144.3 6.2 %collective-permute-start = (f32[16,2,512]{2,0,1:T(8,128)S(1)}, f32[16,2,512]{2,0,1:T(8,128)S(1)}, u32[]{:S(2)}, u32[]{:S(2)}) collective-permute-start(f32[16,2,512]{2,0,1:T(8,128)S(1)} %get-tuple-element.217), channel_id=1, source_target_pairs={{0,4},{4,8},{8,12},{12,16},{16,20},{20,24},{24,28},{1,5},{5,9},{9,... | collective-permute-start | bytes 196616 | tf_op jit(solution)/shard_map/while/body/eval_jaxpr/ppermute | solution.py:26
  164.2 6.2 %collective-permute-start = (f32[16,2,512]{2,0,1:T(8,128)S(1)}, f32[16,2,512]{2,0,1:T(8,128)S(1)}, u32[]{:S(2)}, u32[]{:S(2)}) collective-permute-start(f32[16,2,512]{2,0,1:T(8,128)S(1)} %get-tuple-element.217), channel_id=1, source_target_pairs={{0,4},{4,8},{8,12},{12,16},{16,20},{20,24},{24,28},{1,5},{5,9},{9,... | collective-permute-start | bytes 196616 | tf_op jit(solution)/shard_map/while/body/eval_jaxpr/ppermute | solution.py:26
  181.5 6.8 %collective-permute-start = (f32[16,2,512]{2,0,1:T(8,128)S(1)}, f32[16,2,512]{2,0,1:T(8,128)S(1)}, u32[]{:S(2)}, u32[]{:S(2)}) collective-permute-start(f32[16,2,512]{2,0,1:T(8,128)S(1)} %get-tuple-element.217), channel_id=1, source_target_pairs={{0,4},{4,8},{8,12},{12,16},{16,20},{20,24},{24,28},{1,5},{5,9},{9,... | collective-permute-start | bytes 196616 | tf_op jit(solution)/shard_map/while/body/eval_jaxpr/ppermute | solution.py:26
  199.4 7.1 %collective-permute-start = (f32[16,2,512]{2,0,1:T(8,128)S(1)}, f32[16,2,512]{2,0,1:T(8,128)S(1)}, u32[]{:S(2)}, u32[]{:S(2)}) collective-permute-start(f32[16,2,512]{2,0,1:T(8,128)S(1)} %get-tuple-element.217), channel_id=1, source_target_pairs={{0,4},{4,8},{8,12},{12,16},{16,20},{20,24},{24,28},{1,5},{5,9},{9,... | collective-permute-start | bytes 196616 | tf_op jit(solution)/shard_map/while/body/eval_jaxpr/ppermute | solution.py:26
  217.6 7.1 %collective-permute-start = (f32[16,2,512]{2,0,1:T(8,128)S(1)}, f32[16,2,512]{2,0,1:T(8,128)S(1)}, u32[]{:S(2)}, u32[]{:S(2)}) collective-permute-start(f32[16,2,512]{2,0,1:T(8,128)S(1)} %get-tuple-element.217), channel_id=1, source_target_pairs={{0,4},{4,8},{8,12},{12,16},{16,20},{20,24},{24,28},{1,5},{5,9},{9,... | collective-permute-start | bytes 196616 | tf_op jit(solution)/shard_map/while/body/eval_jaxpr/ppermute | solution.py:26
  235.8 7.1 %collective-permute-start = (f32[16,2,512]{2,0,1:T(8,128)S(1)}, f32[16,2,512]{2,0,1:T(8,128)S(1)}, u32[]{:S(2)}, u32[]{:S(2)}) collective-permute-start(f32[16,2,512]{2,0,1:T(8,128)S(1)} %get-tuple-element.217), channel_id=1, source_target_pairs={{0,4},{4,8},{8,12},{12,16},{16,20},{20,24},{24,28},{1,5},{5,9},{9,... | collective-permute-start | bytes 196616 | tf_op jit(solution)/shard_map/while/body/eval_jaxpr/ppermute | solution.py:26
  254.1 7.1 %collective-permute-start = (f32[16,2,512]{2,0,1:T(8,128)S(1)}, f32[16,2,512]{2,0,1:T(8,128)S(1)}, u32[]{:S(2)}, u32[]{:S(2)}) collective-permute-start(f32[16,2,512]{2,0,1:T(8,128)S(1)} %get-tuple-element.217), channel_id=1, source_target_pairs={{0,4},{4,8},{8,12},{12,16},{16,20},{20,24},{24,28},{1,5},{5,9},{9,... | collective-permute-start | bytes 196616 | tf_op jit(solution)/shard_map/while/body/eval_jaxpr/ppermute | solution.py:26
where the time goes:
time: 278 us; the launch traced here: 273 us
  starting transfers between devices  103 us (37%)
  waiting for transfers between devices  50.3 us (18%)
  matrix products  47.4 us (17%)
  blocking collectives  46.1 us (17%)
  local copies, waits for them, and re-layouts  17.3 us (6%)
  other arithmetic  7.54 us (3%)
    ppermute x16, starting transfers between devices, with_halo(): before = lax.ppermute(last, axis, up)  73.5 us
    dot_general x8, matrix products, fold_rows(): jnp.einsum('fiqj,bqj->bfi', propagator, piece, preferred_element_type=jnp...  47.4 us
    all_gather x7, blocking collectives, turn_receive(): image = add_piece(lax.all_gather(scaled, 'space', axis=2, tiled=True))  40.6 us
    ppermute x7, waiting for transfers between devices, shifted(): lax.ppermute(value, axis, [(source, source + steps) for source in range(l...  38.7 us
    ppermute x16, starting transfers between devices, with_halo(): after = lax.ppermute(leading, axis, down)  20.7 us
    ppermute x16, waiting for transfers between devices, with_halo(): before = lax.ppermute(last, axis, up)  11.6 us
    unnamed x3, local copies, waits for them, and re-layouts  10.7 us
    ppermute x7, starting transfers between devices, shifted(): lax.ppermute(value, axis, [(source, source + steps) for source in range(l...  9.07 us
  transfers between devices with their start and end apart: 39, of which 22 were waited for; matrix products, arithmetic and copies ran while one was open for 5% of the time, Pallas kernels for 0%

commit v1 on v0

v1 whole, which is shorter than its diff:
```python
import functools

import jax
import jax.numpy as jnp
from jax import lax
from jax.experimental import pallas as pl
from jax.experimental.pallas import tpu as pltpu
from jax.sharding import PartitionSpec as P

REFINE = 4
STEPS = 16
LANES = 128
HALF = LANES // 2
CHUNKS = 8
MESH = pl.DeviceIdType.MESH


def kernel(
    cuts, space, x_ref, scl_ref, prop_ref, pipe_ref, fric_ref, out_ref,
    raw, weight, xold, xg, dl, scl, edge, pipes, pipe8, rates,
    raw_sem, old_send, old_recv, edge_send, edge_recv, scl_send, scl_recv,
    dl_send, dl_recv, xg_send, xg_recv,
):
    c = lax.axis_index("cuts")
    s = lax.axis_index("space")
    cl = x_ref.shape[3]
    scen = x_ref.shape[1]
    width = 2 * cl
    rows = raw.shape[0] // CHUNKS
    nv = cl // LANES
    ext = cl + LANES

    raw_copies = [
        pltpu.make_async_copy(
            prop_ref.at[pl.ds(k * rows, rows)], raw.at[pl.ds(k * rows, rows)], raw_sem.at[k]
        )
        for k in range(CHUNKS)
    ]
    for copy in raw_copies:
        copy.start()

    barrier = pltpu.get_barrier_semaphore()
    for d in range(1, space):
        pl.semaphore_signal(
            barrier, inc=1, device_id={"space": lax.rem(s + d, space)}, device_id_type=MESH
        )
    for d in range(1, cuts):
        pl.semaphore_signal(
            barrier, inc=1, device_id={"cuts": lax.rem(c + d, cuts)}, device_id_type=MESH
        )

    for f in range(2):
        xold[s, :, pl.ds(f * cl, cl)] = (scl_ref[0, f, :][None] * x_ref[0, :, f, :]).astype(jnp.bfloat16)
    scl[c] = scl_ref[0]
    pl.semaphore_wait(barrier, space - 1 + cuts - 1)

    right, left = lax.rem(s + 1, space), lax.rem(s + space - 1, space)

    def remote(src, dst, send, recv, **where):
        return pltpu.make_async_remote_copy(
            src_ref=src, dst_ref=dst, send_sem=send, recv_sem=recv, device_id=where, device_id_type=MESH
        )

    edges = [
        remote(pipe_ref, pipes.at[0], edge_send.at[0], edge_recv.at[0], space=right),
        remote(pipe_ref, pipes.at[1], edge_send.at[1], edge_recv.at[1], space=left),
        remote(x_ref.at[0, :, :, pl.ds(cl - LANES, LANES)], edge.at[0], edge_send.at[2], edge_recv.at[2], space=right),
        remote(x_ref.at[0, :, :, pl.ds(0, LANES)], edge.at[1], edge_send.at[3], edge_recv.at[3], space=left),
    ]
    for copy in edges:
        copy.start()
    olds = []
    for d in range(1, space):
        peer = lax.rem(s + d, space)
        olds.append(remote(xold.at[s], xold.at[s], old_send.at[d], old_recv.at[d], space=peer))
        olds[-1].start()

    def scl_copy(slice_id, n):
        return remote(scl_ref.at[0], scl.at[slice_id], scl_send.at[n], scl_recv.at[slice_id], cuts=n)

    def dl_copy(slice_id, n):
        return remote(dl.at[slice_id], dl.at[slice_id], dl_send.at[n], dl_recv.at[slice_id], cuts=n)

    @pl.when(c > 0)
    def _():
        @pl.loop(0, cuts - 1 - c)
        def _(k):
            scl_copy(c, cuts - 1 - k).start()

    fine = REFINE * LANES
    source = lax.broadcasted_iota(jnp.int32, (fine, fine), 0)
    target = lax.broadcasted_iota(jnp.int32, (fine, fine), 1)
    pick = source == REFINE * (target % LANES) + target // LANES
    for copy in edges[:2]:
        copy.wait()
    pipe8[...] = jnp.zeros_like(pipe8)
    pipe8[pl.ds(0, nv)] = pipe_ref[...]
    pipe8[pl.ds(nv, 1)] = pipes[1, pl.ds(0, 1)]
    pipe8[pl.ds(nv + 1, 1)] = pipes[0, pl.ds(nv - 1, 1)]
    phased = jnp.dot(
        pipe8[...].astype(jnp.float32).astype(jnp.bfloat16),
        pick.astype(jnp.float32).astype(jnp.bfloat16),
        preferred_element_type=jnp.float32,
    )
    rate8 = jnp.zeros(phased.shape, jnp.float32)
    for k in range(fric_ref.shape[0]):
        rate8 = jnp.where(phased == float(k), fric_ref[k], rate8)
    near = lax.broadcasted_iota(jnp.int32, (1, LANES), 1) < HALF
    for r in range(REFINE):
        part = rate8[:, r * LANES : (r + 1) * LANES]
        for v in range(nv):
            rates[r, :, pl.ds(v * LANES, LANES)] = jnp.broadcast_to(part[v : v + 1], (scen, LANES))
        halo = jnp.where(near, part[nv : nv + 1], part[nv + 1 : nv + 2])
        rates[r, :, pl.ds(cl, LANES)] = jnp.broadcast_to(halo, (scen, LANES))

    for copy in edges[2:]:
        copy.wait()
    lane = lax.broadcasted_iota(jnp.int32, (1, ext), 1)
    has_right = (s < space - 1).astype(jnp.float32)
    has_left = (s > 0).astype(jnp.float32)
    keep = jnp.where(lane < cl, 1.0, jnp.where(lane < cl + HALF, has_right, has_left))

    def extended(f):
        halo = jnp.where(near, edge[1, :, f, :], edge[0, :, f, :])
        return keep * jnp.concatenate([x_ref[0, :, f, :], halo], axis=1)

    head, flow = extended(0), extended(1)

    def sweep(_, state):
        fwd, bwd = state
        drag = []
        for r in range(REFINE):
            q = 0.5 * (fwd[r] - bwd[r])
            drag.append(q * jnp.abs(q))
        fwd_new, bwd_new = [], []
        for r in range(REFINE):
            rate = rates[r]
            if r > 0:
                prev_f, prev_d = fwd[r - 1], drag[r - 1]
            else:
                prev_f, prev_d = pltpu.roll(fwd[-1], 1, 1), pltpu.roll(drag[-1], 1, 1)
            if r < REFINE - 1:
                next_b, next_d = bwd[r + 1], drag[r + 1]
            else:
                next_b, next_d = pltpu.roll(bwd[0], ext - 1, 1), pltpu.roll(drag[0], ext - 1, 1)
            fwd_new.append(keep * (prev_f - rate * prev_d))
            bwd_new.append(keep * (next_b + rate * next_d))
        return tuple(fwd_new), tuple(bwd_new)

    fwd, bwd = lax.fori_loop(
        0, STEPS, sweep, ((head + flow,) * REFINE, (head - flow,) * REFINE)
    )
    fwd_sum = (fwd[0] + fwd[1] + fwd[2] + fwd[3])[:, :cl]
    bwd_sum = (bwd[0] + bwd[1] + bwd[2] + bwd[3])[:, :cl]
    share = 0.5 / REFINE
    dl[c, :, pl.ds(0, cl)] = share * (fwd_sum + bwd_sum)
    dl[c, :, pl.ds(cl, cl)] = share * (fwd_sum - bwd_sum)

    def send_delta():
        @pl.loop(0, cuts - 1 - c)
        def _(k):
            dl_copy(c, cuts - 1 - k).start()

    @pl.when(c == 0)
    def _():
        send_delta()

    for k, copy in enumerate(raw_copies):
        copy.wait()
        at = pl.ds(k * rows, rows)
        for t in range(space):
            for q in range(2):
                weight[t, at, pl.ds(q * cl, cl)] = raw[at, q, pl.ds(t * cl, cl)]

    def apply_piece(piece, t):
        return lax.dot_general(
            piece, weight[t], (((1,), (1,)), ((), ())), preferred_element_type=jnp.float32
        )

    for copy in olds:
        copy.wait()

    @pl.when(c > 0)
    def _():
        image = apply_piece(xold[0], 0)
        for t in range(1, space):
            image += apply_piece(xold[t], t)
        dl[c] = dl[c] - image
        send_delta()

    def advance(m, image):
        slot = lax.rem(m, 2)
        remote(dl.at[m], dl.at[m], dl_send.at[m], dl_recv.at[m], cuts=m).wait_recv()

        @pl.when(m + 1 < c)
        def _():
            scl_copy(m + 1, m + 1).wait_recv()

        state = image + dl[m]
        for f in range(2):
            at = pl.ds(f * cl, cl)
            xg[slot, s, :, at] = (scl[m + 1, f, :][None] * state[:, f * cl : (f + 1) * cl]).astype(jnp.bfloat16)
        copies = []
        for d in range(1, space):
            peer = lax.bitwise_xor(s, d)
            copies.append(
                remote(xg.at[slot, s], xg.at[slot, s], xg_send.at[slot, d], xg_recv.at[slot, d], space=peer)
            )
            copies[-1].start()
        total = apply_piece(xg[slot, s], s)
        for d in range(1, space):
            copies[d - 1].wait_recv()
            peer = lax.bitwise_xor(s, d)
            total += apply_piece(xg[slot, peer], peer)
        for copy in copies:
            copy.wait_send()
        return total

    image = lax.fori_loop(0, c, advance, jnp.zeros((scen, width), jnp.float32))
    out_ref[...] = image + dl[c]

    @pl.loop(0, cuts - 1 - c)
    def _(k):
        dl_copy(c, cuts - 1 - k).wait_send()

    @pl.when(c > 0)
    def _():
        @pl.loop(0, cuts - 1 - c)
        def _(k):
            scl_copy(c, cuts - 1 - k).wait_send()


def solution(mesh):
    cuts, space = mesh.shape["cuts"], mesh.shape["space"]

    def local(start_old, scales, propagator, pipe_of_cell, friction):
        scen, cl = start_old.shape[1], start_old.shape[3]
        cells = propagator.shape[3]
        width = 2 * cl
        fine = REFINE * LANES
        pipes = pipe_of_cell.reshape(-1, fine)
        nv = pipes.shape[0]
        vmem = pl.BlockSpec(memory_space=pltpu.VMEM)
        dma = pltpu.SemaphoreType.DMA
        out = pl.pallas_call(
            functools.partial(kernel, cuts, space),
            out_shape=jax.ShapeDtypeStruct((scen, width), jnp.float32),
            in_specs=[vmem, vmem, pl.BlockSpec(memory_space=pl.ANY), vmem, pl.BlockSpec(memory_space=pltpu.SMEM)],
            out_specs=vmem,
            scratch_shapes=[
                pltpu.VMEM((width, 2, cells), jnp.bfloat16),
                pltpu.VMEM((space, width, width), jnp.bfloat16),
                pltpu.VMEM((space, scen, width), jnp.bfloat16),
                pltpu.VMEM((2, space, scen, width), jnp.bfloat16),
                pltpu.VMEM((cuts, scen, width), jnp.float32),
                pltpu.VMEM((cuts, 2, cl), jnp.float32),
                pltpu.VMEM((2, scen, 2, LANES), jnp.float32),
                pltpu.VMEM((2, nv, fine), jnp.int32),
                pltpu.VMEM((8, fine), jnp.int32),
                pltpu.VMEM((REFINE, scen, cl + LANES), jnp.float32),
                dma((CHUNKS,)),
                dma((space,)), dma((space,)),
                dma((4,)), dma((4,)),
                dma((cuts,)), dma((cuts,)),
                dma((cuts,)), dma((cuts,)),
                dma((2, space)), dma((2, space)),
            ],
            compiler_params=pltpu.CompilerParams(
                collective_id=0, has_side_effects=True, vmem_limit_bytes=48 * 2**20
            ),
        )(start_old, scales, propagator.reshape(width, 2, cells), pipes, friction)
        return out.reshape(1, scen, 2, cl)

    placed = (
        P("cuts", None, None, "space"),
        P("cuts", None, "space"),
        P(None, "space", None, None),
        P("space"),
        P(),
    )
    return jax.shard_map(
        local, mesh=mesh, in_specs=placed, out_specs=P("cuts", None, None, "space"), check_vma=False
    )
```

time: 278 us -> 61.2 us (0.22); the launches traced: 273 us -> 60.9 us
  starting transfers between devices: 103 us -> 0 us
  Pallas kernels: 0 us -> 57.3 us
  waiting for transfers between devices: 50.3 us -> 0 us
  matrix products: 47.4 us -> 0 us
  blocking collectives: 46.1 us -> 0 us
  local copies, waits for them, and re-layouts: 17.3 us -> 3.57 us
  other arithmetic: 7.54 us -> 0 us
    ppermute x39 -> x0, starting transfers between devices: 103 us -> none  [the longest x16 73.5 us: with_halo(): before = lax.ppermute(last, axis, up)]
    pallas_call x0 -> x1, Pallas kernels: none -> 57.3 us  [local(): pl.pallas_call(functools.partial(kernel, cuts, space), out_shape=jax.Shap...]
    ppermute x39 -> x0, waiting for transfers between devices: 50.3 us -> none  [the longest x7 38.7 us: shifted(): lax.ppermute(value, axis, [(source, source + steps) for source in range(l...]
    dot_general x8 -> x0, matrix products: 47.4 us -> none  [fold_rows(): jnp.einsum('fiqj,bqj->bfi', propagator, piece, preferred_element_type=jnp...]
    all_gather x8 -> x0, blocking collectives: 46.1 us -> none  [the longest x7 40.6 us: turn_receive(): image = add_piece(lax.all_gather(scaled, 'space', axis=2, tiled=True))]
    unnamed x3 -> x6, local copies, waits for them, and re-layouts: 10.7 us -> 2.18 us
    another operation x45 -> x0, other arithmetic: 3.51 us -> none  [local(): field = jnp.stack([head, flow], axis=1)]
    reduce_sum x2 -> x0, other arithmetic: 2.97 us -> none  [the longest x1 1.63 us: local(): jnp.mean(field.reshape(scen_count, 2, coarse_local, REFINE), axis=-1)]
  transfers between devices with their start and end apart: 39 -> 0, of which waited for: 22 -> 0; matrix products, arithmetic and copies ran while one was open for 5% -> 0% of each run, Pallas kernels for 0% -> 0%
where the time goes in v1:
time: 61.2 us; the launch traced here: 60.9 us
  Pallas kernels  57.3 us (94%)
  local copies, waits for them, and re-layouts  3.57 us (6%)
    pallas_call x1, Pallas kernels, local(): pl.pallas_call(functools.partial(kernel, cuts, space), out_shape=jax.Shap...  57.3 us
    unnamed x6, local copies, waits for them, and re-layouts  2.18 us

profile of v1, /device:TPU:26, one launch (start us, length us, event | category | flops | bytes accessed | tf_op | source)
XLA Modules:
  0.0 60.9 jit_solution(17758417817153783451)
XLA Ops:
  0.0 0.7 %reshape.10.pipe_ref = s32[4,512]{1,0:T(4,128)S(1)} reshape(s32[2048]{0:T(1024)} %param.8) | data formatting | bytes 16384 | tf_op jit(solution)/shard_map/reshape | solution.py:241
  0.7 0.0 copy-start
  0.7 0.8 %copy-done = f32[1,16,2,512]{3,2,1,0:T(2,128)S(1)} copy-done((f32[1,16,2,512]{3,2,1,0:T(2,128)S(1)}, f32[1,16,2,512]{3,2,1,0:T(2,128)}, u32[]{:S(2)}) %copy-start) | copy-done | bytes 65560
  1.5 0.0 copy-start.1
  1.5 0.7 %copy-done.1 = f32[1,2,512]{2,1,0:T(2,128)S(1)} copy-done((f32[1,2,512]{2,1,0:T(2,128)S(1)}, f32[1,2,512]{2,1,0:T(2,128)}, u32[]{:S(2)}) %copy-start.1) | copy-done | bytes 4120
  2.2 0.0 copy-start.2
  2.2 0.7 %copy-done.2 = f32[128]{0:T(128)S(1)} copy-done((f32[128]{0:T(128)S(1)}, f32[128]{0:T(128)}, u32[]{:S(2)}) %copy-start.2) | copy-done | bytes 536
  2.9 57.3 %shard_map.55 = f32[16,1024]{1,0:T(8,128)S(1)} custom-call(f32[1,16,2,512]{3,2,1,0:T(2,128)S(1)} %copy-done, f32[1,2,512]{2,1,0:T(2,128)S(1)} %copy-done.1, bf16[1024,2,2048]{2,1,0:T(2,128)(2,1)} %bitcast.1, s32[4,512]{1,0:T(4,128)S(1)} %reshape.10.pipe_ref, f32[128]{0:T(128)S(1)} %copy-done.2), custom_call_target="tpu_custom_call" | custom-call | tf_op jit(solution)/shard_map/pallas_call | solution.py:245
  60.2 0.7 %reshape.11 = f32[1,16,2,512]{3,2,1,0:T(2,128)} reshape(f32[16,1024]{1,0:T(8,128)S(1)} %shard_map.55) | data formatting | bytes 131072 | tf_op jit(solution)/shard_map/reshape | solution.py:272
Async XLA Ops:
  0.7 0.8 %copy-start = (f32[1,16,2,512]{3,2,1,0:T(2,128)S(1)}, f32[1,16,2,512]{3,2,1,0:T(2,128)}, u32[]{:S(2)}) copy-start(f32[1,16,2,512]{3,2,1,0:T(2,128)} %x_ref.1) | copy-start | bytes 196612
  1.5 0.7 %copy-start.1 = (f32[1,2,512]{2,1,0:T(2,128)S(1)}, f32[1,2,512]{2,1,0:T(2,128)}, u32[]{:S(2)}) copy-start(f32[1,2,512]{2,1,0:T(2,128)} %scl_ref.1) | copy-start | bytes 12292
  2.2 0.7 %copy-start.2 = (f32[128]{0:T(128)S(1)}, f32[128]{0:T(128)}, u32[]{:S(2)}) copy-start(f32[128]{0:T(128)} %fric_ref.1) | copy-start | bytes 1540

commit v2 on v1

--- a/solution.py
+++ b/solution.py
@@ -11,7 +11,7 @@
 STEPS = 16
 LANES = 128
 HALF = LANES // 2
-CHUNKS = 8
+ROWS = 128
 MESH = pl.DeviceIdType.MESH
 
 
@@ -26,18 +26,15 @@
     cl = x_ref.shape[3]
     scen = x_ref.shape[1]
     width = 2 * cl
-    rows = raw.shape[0] // CHUNKS
     nv = cl // LANES
     ext = cl + LANES
 
-    raw_copies = [
-        pltpu.make_async_copy(
-            prop_ref.at[pl.ds(k * rows, rows)], raw.at[pl.ds(k * rows, rows)], raw_sem.at[k]
-        )
-        for k in range(CHUNKS)
-    ]
-    for copy in raw_copies:
-        copy.start()
+    def raw_copy(k):
+        at = pl.ds(pl.multiple_of(k * ROWS, ROWS), ROWS)
+        return pltpu.make_async_copy(prop_ref.at[at], raw.at[at], raw_sem.at[k])
+
+    for k in range(raw.shape[0] // ROWS):
+        raw_copy(k).start()
 
     barrier = pltpu.get_barrier_semaphore()
     for d in range(1, space):
@@ -148,7 +145,7 @@
         return tuple(fwd_new), tuple(bwd_new)
 
     fwd, bwd = lax.fori_loop(
-        0, STEPS, sweep, ((head + flow,) * REFINE, (head - flow,) * REFINE)
+        0, STEPS, sweep, ((head + flow,) * REFINE, (head - flow,) * REFINE), unroll=True
     )
     fwd_sum = (fwd[0] + fwd[1] + fwd[2] + fwd[3])[:, :cl]
     bwd_sum = (bwd[0] + bwd[1] + bwd[2] + bwd[3])[:, :cl]
@@ -165,16 +162,18 @@
     def _():
         send_delta()
 
-    for k, copy in enumerate(raw_copies):
-        copy.wait()
-        at = pl.ds(k * rows, rows)
-        for t in range(space):
-            for q in range(2):
-                weight[t, at, pl.ds(q * cl, cl)] = raw[at, q, pl.ds(t * cl, cl)]
+    @pl.loop(0, raw.shape[0] // ROWS)
+    def _(k):
+        at = pl.ds(pl.multiple_of(k * ROWS, ROWS), ROWS)
+        raw_copy(k).wait()
+        fields = pltpu.einshape("rqj->qrj", raw[at])
+        for q in range(2):
+            for t in range(space):
+                weight[t, pl.ds(q * cl, cl), at] = fields[q][:, t * cl : (t + 1) * cl].T
 
     def apply_piece(piece, t):
         return lax.dot_general(
-            piece, weight[t], (((1,), (1,)), ((), ())), preferred_element_type=jnp.float32
+            piece, weight[t], (((1,), (0,)), ((), ())), preferred_element_type=jnp.float32
         )
 
     for copy in olds:
@@ -258,7 +257,7 @@
                 pltpu.VMEM((2, nv, fine), jnp.int32),
                 pltpu.VMEM((8, fine), jnp.int32),
                 pltpu.VMEM((REFINE, scen, cl + LANES), jnp.float32),
-                dma((CHUNKS,)),
+                dma((width // ROWS,)),
                 dma((space,)), dma((space,)),
                 dma((4,)), dma((4,)),
                 dma((cuts,)), dma((cuts,)),

time: 61.2 us -> 43 us (0.70)
  Pallas kernels: 57.3 us -> 39.1 us
    pallas_call x1, Pallas kernels: 57.3 us -> 39.1 us  [local(): pl.pallas_call(functools.partial(kernel, cuts, space), out_shape=jax.Shap...]
where the time goes in v2:
time: 43 us; the launch traced here: 42.7 us
  Pallas kernels  39.1 us (91%)
  local copies, waits for them, and re-layouts  3.57 us (8%)
    pallas_call x1, Pallas kernels, local(): pl.pallas_call(functools.partial(kernel, cuts, space), out_shape=jax.Shap...  39.1 us
    unnamed x6, local copies, waits for them, and re-layouts  2.18 us

profile of v2, /device:TPU:26, one launch (start us, length us, event | category | flops | bytes accessed | tf_op | source)
XLA Modules:
  0.0 42.7 jit_solution(13639187358263057464)
XLA Ops:
  0.0 0.7 %reshape.10.pipe_ref = s32[4,512]{1,0:T(4,128)S(1)} reshape(s32[2048]{0:T(1024)} %param.8) | data formatting | bytes 16384 | tf_op jit(solution)/shard_map/reshape | solution.py:240
  0.7 0.0 copy-start
  0.7 0.8 %copy-done = f32[1,16,2,512]{3,2,1,0:T(2,128)S(1)} copy-done((f32[1,16,2,512]{3,2,1,0:T(2,128)S(1)}, f32[1,16,2,512]{3,2,1,0:T(2,128)}, u32[]{:S(2)}) %copy-start) | copy-done | bytes 65560
  1.5 0.0 copy-start.1
  1.5 0.7 %copy-done.1 = f32[1,2,512]{2,1,0:T(2,128)S(1)} copy-done((f32[1,2,512]{2,1,0:T(2,128)S(1)}, f32[1,2,512]{2,1,0:T(2,128)}, u32[]{:S(2)}) %copy-start.1) | copy-done | bytes 4120
  2.2 0.0 copy-start.2
  2.2 0.7 %copy-done.2 = f32[128]{0:T(128)S(1)} copy-done((f32[128]{0:T(128)S(1)}, f32[128]{0:T(128)}, u32[]{:S(2)}) %copy-start.2) | copy-done | bytes 536
  2.9 39.1 %shard_map.55 = f32[16,1024]{1,0:T(8,128)S(1)} custom-call(f32[1,16,2,512]{3,2,1,0:T(2,128)S(1)} %copy-done, f32[1,2,512]{2,1,0:T(2,128)S(1)} %copy-done.1, bf16[1024,2,2048]{2,1,0:T(2,128)(2,1)} %bitcast.1, s32[4,512]{1,0:T(4,128)S(1)} %reshape.10.pipe_ref, f32[128]{0:T(128)S(1)} %copy-done.2), custom_call_target="tpu_custom_call" | custom-call | tf_op jit(solution)/shard_map/pallas_call | solution.py:244
  42.0 0.7 %reshape.11 = f32[1,16,2,512]{3,2,1,0:T(2,128)} reshape(f32[16,1024]{1,0:T(8,128)S(1)} %shard_map.55) | data formatting | bytes 131072 | tf_op jit(solution)/shard_map/reshape | solution.py:271
Async XLA Ops:
  0.7 0.8 %copy-start = (f32[1,16,2,512]{3,2,1,0:T(2,128)S(1)}, f32[1,16,2,512]{3,2,1,0:T(2,128)}, u32[]{:S(2)}) copy-start(f32[1,16,2,512]{3,2,1,0:T(2,128)} %x_ref.1) | copy-start | bytes 196612
  1.5 0.7 %copy-start.1 = (f32[1,2,512]{2,1,0:T(2,128)S(1)}, f32[1,2,512]{2,1,0:T(2,128)}, u32[]{:S(2)}) copy-start(f32[1,2,512]{2,1,0:T(2,128)} %scl_ref.1) | copy-start | bytes 12292
  2.2 0.7 %copy-start.2 = (f32[128]{0:T(128)S(1)}, f32[128]{0:T(128)}, u32[]{:S(2)}) copy-start(f32[128]{0:T(128)} %fric_ref.1) | copy-start | bytes 1540

commit v3 on v2

--- a/solution.py
+++ b/solution.py
@@ -1,4 +1,5 @@
 import functools
+import math
 
 import jax
 import jax.numpy as jnp
@@ -17,9 +18,9 @@
 
 def kernel(
     cuts, space, x_ref, scl_ref, prop_ref, pipe_ref, fric_ref, out_ref,
-    raw, weight, xold, xg, dl, scl, edge, pipes, pipe8, rates,
+    raw, weight, xold, xg, own, dl, res_out, res_in, scl, edge, pipes, pipe8, rates,
     raw_sem, old_send, old_recv, edge_send, edge_recv, scl_send, scl_recv,
-    dl_send, dl_recv, xg_send, xg_recv,
+    dl_send, dl_recv, xg_send, xg_recv, res_send, res_recv,
 ):
     c = lax.axis_index("cuts")
     s = lax.axis_index("space")
@@ -28,6 +29,8 @@
     width = 2 * cl
     nv = cl // LANES
     ext = cl + LANES
+    parts, share_rows = own.shape[0], own.shape[1]
+    part, rep, reps = lax.rem(c, parts), lax.div(c, parts), cuts // parts
 
     def raw_copy(k):
         at = pl.ds(pl.multiple_of(k * ROWS, ROWS), ROWS)
@@ -76,13 +79,19 @@
         return remote(scl_ref.at[0], scl.at[slice_id], scl_send.at[n], scl_recv.at[slice_id], cuts=n)
 
     def dl_copy(slice_id, n):
-        return remote(dl.at[slice_id], dl.at[slice_id], dl_send.at[n], dl_recv.at[slice_id], cuts=n)
+        return remote(own.at[lax.rem(n, parts)], dl.at[slice_id], dl_send.at[n], dl_recv.at[slice_id], cuts=n)
+
+    def res_copy(n):
+        return remote(res_out.at[n], res_in.at[part], res_send.at[n], res_recv.at[part], cuts=n)
+
+    def other(k):
+        return lax.rem(c + cuts - 1 - k, cuts)
 
     @pl.when(c > 0)
     def _():
-        @pl.loop(0, cuts - 1 - c)
+        @pl.loop(0, cuts - 1)
         def _(k):
-            scl_copy(c, cuts - 1 - k).start()
+            scl_copy(c, other(k)).start()
 
     fine = REFINE * LANES
     source = lax.broadcasted_iota(jnp.int32, (fine, fine), 0)
@@ -104,10 +113,10 @@
         rate8 = jnp.where(phased == float(k), fric_ref[k], rate8)
     near = lax.broadcasted_iota(jnp.int32, (1, LANES), 1) < HALF
     for r in range(REFINE):
-        part = rate8[:, r * LANES : (r + 1) * LANES]
+        block = rate8[:, r * LANES : (r + 1) * LANES]
         for v in range(nv):
-            rates[r, :, pl.ds(v * LANES, LANES)] = jnp.broadcast_to(part[v : v + 1], (scen, LANES))
-        halo = jnp.where(near, part[nv : nv + 1], part[nv + 1 : nv + 2])
+            rates[r, :, pl.ds(v * LANES, LANES)] = jnp.broadcast_to(block[v : v + 1], (scen, LANES))
+        halo = jnp.where(near, block[nv : nv + 1], block[nv + 1 : nv + 2])
         rates[r, :, pl.ds(cl, LANES)] = jnp.broadcast_to(halo, (scen, LANES))
 
     for copy in edges[2:]:
@@ -150,17 +159,20 @@
     fwd_sum = (fwd[0] + fwd[1] + fwd[2] + fwd[3])[:, :cl]
     bwd_sum = (bwd[0] + bwd[1] + bwd[2] + bwd[3])[:, :cl]
     share = 0.5 / REFINE
-    dl[c, :, pl.ds(0, cl)] = share * (fwd_sum + bwd_sum)
-    dl[c, :, pl.ds(cl, cl)] = share * (fwd_sum - bwd_sum)
-
-    def send_delta():
-        @pl.loop(0, cuts - 1 - c)
+    fine_coarse = jnp.concatenate([share * (fwd_sum + bwd_sum), share * (fwd_sum - bwd_sum)], axis=1)
+
+    def send_delta(delta):
+        for p in range(parts):
+            own[p] = delta[p * share_rows : (p + 1) * share_rows]
+        dl[c] = own[part]
+
+        @pl.loop(0, cuts - 1)
         def _(k):
-            dl_copy(c, cuts - 1 - k).start()
+            dl_copy(c, other(k)).start()
 
     @pl.when(c == 0)
     def _():
-        send_delta()
+        send_delta(fine_coarse)
 
     @pl.loop(0, raw.shape[0] // ROWS)
     def _(k):
@@ -184,49 +196,90 @@
         image = apply_piece(xold[0], 0)
         for t in range(1, space):
             image += apply_piece(xold[t], t)
-        dl[c] = dl[c] - image
-        send_delta()
+        send_delta(fine_coarse - image)
+
+    def slice_end(m, image):
+        @pl.when(m != c)
+        def _():
+            dl_copy(m, m).wait_recv()
+
+        return image + dl[m]
+
+    def hand_over(m, state):
+        mine = jnp.logical_and(m > 0, lax.rem(m, reps) == rep)
+
+        @pl.when(jnp.logical_and(mine, m == c))
+        def _():
+            res_in[part] = state
+
+        @pl.when(jnp.logical_and(mine, m != c))
+        def _():
+            res_out[m] = state
+            res_copy(m).start()
 
     def advance(m, image):
         slot = lax.rem(m, 2)
-        remote(dl.at[m], dl.at[m], dl_send.at[m], dl_recv.at[m], cuts=m).wait_recv()
-
-        @pl.when(m + 1 < c)
+
+        @pl.when(m + 1 != c)
         def _():
             scl_copy(m + 1, m + 1).wait_recv()
 
-        state = image + dl[m]
+        state = slice_end(m, image)
         for f in range(2):
             at = pl.ds(f * cl, cl)
             xg[slot, s, :, at] = (scl[m + 1, f, :][None] * state[:, f * cl : (f + 1) * cl]).astype(jnp.bfloat16)
         copies = []
-        for d in range(1, space):
+        for d in reversed(range(1, space)):
             peer = lax.bitwise_xor(s, d)
             copies.append(
                 remote(xg.at[slot, s], xg.at[slot, s], xg_send.at[slot, d], xg_recv.at[slot, d], space=peer)
             )
             copies[-1].start()
+        hand_over(m, state)
         total = apply_piece(xg[slot, s], s)
         for d in range(1, space):
-            copies[d - 1].wait_recv()
+            copies[space - 1 - d].wait_recv()
             peer = lax.bitwise_xor(s, d)
             total += apply_piece(xg[slot, peer], peer)
         for copy in copies:
             copy.wait_send()
         return total
 
-    image = lax.fori_loop(0, c, advance, jnp.zeros((scen, width), jnp.float32))
-    out_ref[...] = image + dl[c]
-
-    @pl.loop(0, cuts - 1 - c)
+    image = lax.fori_loop(0, cuts - 1, advance, jnp.zeros((share_rows, width), jnp.float32))
+    hand_over(cuts - 1, slice_end(cuts - 1, image))
+
+    def write(source):
+        for p in range(parts):
+            for f in range(2):
+                out_ref[pl.ds(p * share_rows, share_rows), pl.ds(f * cl, cl)] = source[p, :, pl.ds(f * cl, cl)]
+
+    @pl.when(c == 0)
+    def _():
+        write(own)
+
+    @pl.when(c > 0)
+    def _():
+        for p in range(parts):
+            holder = lax.rem(c, reps) * parts + p
+
+            @pl.when(holder != c)
+            def _():
+                remote(res_out.at[c], res_in.at[p], res_send.at[c], res_recv.at[p], cuts=holder).wait_recv()
+
+        write(res_in)
+
+    @pl.loop(0, cuts - 1)
     def _(k):
-        dl_copy(c, cuts - 1 - k).wait_send()
-
-    @pl.when(c > 0)
-    def _():
-        @pl.loop(0, cuts - 1 - c)
-        def _(k):
-            scl_copy(c, cuts - 1 - k).wait_send()
+        n = other(k)
+        dl_copy(c, n).wait_send()
+
+        @pl.when(c > 0)
+        def _():
+            scl_copy(c, n).wait_send()
+
+        @pl.when(jnp.logical_and(n > 0, lax.rem(n, reps) == rep))
+        def _():
+            res_copy(n).wait_send()
 
 
 def solution(mesh):
@@ -236,6 +289,7 @@
         scen, cl = start_old.shape[1], start_old.shape[3]
         cells = propagator.shape[3]
         width = 2 * cl
+        parts = math.gcd(cuts, scen)
         fine = REFINE * LANES
         pipes = pipe_of_cell.reshape(-1, fine)
         nv = pipes.shape[0]
@@ -250,8 +304,11 @@
                 pltpu.VMEM((width, 2, cells), jnp.bfloat16),
                 pltpu.VMEM((space, width, width), jnp.bfloat16),
                 pltpu.VMEM((space, scen, width), jnp.bfloat16),
-                pltpu.VMEM((2, space, scen, width), jnp.bfloat16),
-                pltpu.VMEM((cuts, scen, width), jnp.float32),
+                pltpu.VMEM((2, space, scen // parts, width), jnp.bfloat16),
+                pltpu.VMEM((parts, scen // parts, width), jnp.float32),
+                pltpu.VMEM((cuts, scen // parts, width), jnp.float32),
+                pltpu.VMEM((cuts, scen // parts, width), jnp.float32),
+                pltpu.VMEM((parts, scen // parts, width), jnp.float32),
                 pltpu.VMEM((cuts, 2, cl), jnp.float32),
                 pltpu.VMEM((2, scen, 2, LANES), jnp.float32),
                 pltpu.VMEM((2, nv, fine), jnp.int32),
@@ -263,6 +320,7 @@
                 dma((cuts,)), dma((cuts,)),
                 dma((cuts,)), dma((cuts,)),
                 dma((2, space)), dma((2, space)),
+                dma((cuts,)), dma((parts,)),
             ],
             compiler_params=pltpu.CompilerParams(
                 collective_id=0, has_side_effects=True, vmem_limit_bytes=48 * 2**20

time: 43 us -> 43.8 us (1.019); the launches traced: 42.7 us -> 43 us
  no operation moved by 1% of the time
where the time goes in v3:
time: 43.8 us; the launch traced here: 43 us
  Pallas kernels  39.4 us (90%)
  local copies, waits for them, and re-layouts  3.57 us (8%)
    pallas_call x1, Pallas kernels, local(): pl.pallas_call(functools.partial(kernel, cuts, space), out_shape=jax.Shap...  39.4 us
    unnamed x6, local copies, waits for them, and re-layouts  2.18 us

profile of v3, /device:TPU:26, one launch (start us, length us, event | category | flops | bytes accessed | tf_op | source)
XLA Modules:
  0.0 43.0 jit_solution(3551378598101535362)
XLA Ops:
  0.0 0.7 %reshape.10.pipe_ref = s32[4,512]{1,0:T(4,128)S(1)} reshape(s32[2048]{0:T(1024)} %param.8) | data formatting | bytes 16384 | tf_op jit(solution)/shard_map/reshape | solution.py:294
  0.7 0.0 copy-start
  0.7 0.8 %copy-done = f32[1,16,2,512]{3,2,1,0:T(2,128)S(1)} copy-done((f32[1,16,2,512]{3,2,1,0:T(2,128)S(1)}, f32[1,16,2,512]{3,2,1,0:T(2,128)}, u32[]{:S(2)}) %copy-start) | copy-done | bytes 65560
  1.5 0.0 copy-start.1
  1.5 0.7 %copy-done.1 = f32[1,2,512]{2,1,0:T(2,128)S(1)} copy-done((f32[1,2,512]{2,1,0:T(2,128)S(1)}, f32[1,2,512]{2,1,0:T(2,128)}, u32[]{:S(2)}) %copy-start.1) | copy-done | bytes 4120
  2.2 0.0 copy-start.2
  2.2 0.7 %copy-done.2 = f32[128]{0:T(128)S(1)} copy-done((f32[128]{0:T(128)S(1)}, f32[128]{0:T(128)}, u32[]{:S(2)}) %copy-start.2) | copy-done | bytes 536
  2.9 39.4 %shard_map.55 = f32[16,1024]{1,0:T(8,128)S(1)} custom-call(f32[1,16,2,512]{3,2,1,0:T(2,128)S(1)} %copy-done, f32[1,2,512]{2,1,0:T(2,128)S(1)} %copy-done.1, bf16[1024,2,2048]{2,1,0:T(2,128)(2,1)} %bitcast.1, s32[4,512]{1,0:T(4,128)S(1)} %reshape.10.pipe_ref, f32[128]{0:T(128)S(1)} %copy-done.2), custom_call_target="tpu_custom_call" | custom-call | tf_op jit(solution)/shard_map/pallas_call | solution.py:298
  42.3 0.7 %reshape.11 = f32[1,16,2,512]{3,2,1,0:T(2,128)} reshape(f32[16,1024]{1,0:T(8,128)S(1)} %shard_map.55) | data formatting | bytes 131072 | tf_op jit(solution)/shard_map/reshape | solution.py:329
Async XLA Ops:
  0.7 0.8 %copy-start = (f32[1,16,2,512]{3,2,1,0:T(2,128)S(1)}, f32[1,16,2,512]{3,2,1,0:T(2,128)}, u32[]{:S(2)}) copy-start(f32[1,16,2,512]{3,2,1,0:T(2,128)} %x_ref.1) | copy-start | bytes 196612
  1.5 0.7 %copy-start.1 = (f32[1,2,512]{2,1,0:T(2,128)S(1)}, f32[1,2,512]{2,1,0:T(2,128)}, u32[]{:S(2)}) copy-start(f32[1,2,512]{2,1,0:T(2,128)} %scl_ref.1) | copy-start | bytes 12292
  2.2 0.7 %copy-start.2 = (f32[128]{0:T(128)S(1)}, f32[128]{0:T(128)}, u32[]{:S(2)}) copy-start(f32[128]{0:T(128)} %fric_ref.1) | copy-start | bytes 1540

commit v4 on v3

--- a/solution.py
+++ b/solution.py
@@ -52,6 +52,19 @@
     for f in range(2):
         xold[s, :, pl.ds(f * cl, cl)] = (scl_ref[0, f, :][None] * x_ref[0, :, f, :]).astype(jnp.bfloat16)
     scl[c] = scl_ref[0]
+    chunks = raw.shape[0] // ROWS
+
+    def rearrange(first, stop):
+        @pl.loop(first, stop)
+        def _(k):
+            at = pl.ds(pl.multiple_of(k * ROWS, ROWS), ROWS)
+            raw_copy(k).wait()
+            fields = pltpu.einshape("rqj->qrj", raw[at])
+            for q in range(2):
+                for t in range(space):
+                    weight[t, pl.ds(q * cl, cl), at] = fields[q][:, t * cl : (t + 1) * cl].T
+
+    rearrange(0, chunks // 2)
     pl.semaphore_wait(barrier, space - 1 + cuts - 1)
 
     right, left = lax.rem(s + 1, space), lax.rem(s + space - 1, space)
@@ -92,6 +105,8 @@
         @pl.loop(0, cuts - 1)
         def _(k):
             scl_copy(c, other(k)).start()
+
+    rearrange(chunks // 2, chunks)
 
     fine = REFINE * LANES
     source = lax.broadcasted_iota(jnp.int32, (fine, fine), 0)
@@ -173,15 +188,6 @@
     @pl.when(c == 0)
     def _():
         send_delta(fine_coarse)
-
-    @pl.loop(0, raw.shape[0] // ROWS)
-    def _(k):
-        at = pl.ds(pl.multiple_of(k * ROWS, ROWS), ROWS)
-        raw_copy(k).wait()
-        fields = pltpu.einshape("rqj->qrj", raw[at])
-        for q in range(2):
-            for t in range(space):
-                weight[t, pl.ds(q * cl, cl), at] = fields[q][:, t * cl : (t + 1) * cl].T
 
     def apply_piece(piece, t):
         return lax.dot_general(

time: 43.8 us -> 42.1 us (0.961); the launches traced: 43 us -> 41.8 us
  Pallas kernels: 39.4 us -> 38.2 us
    pallas_call x1, Pallas kernels: 39.4 us -> 38.2 us  [local(): pl.pallas_call(functools.partial(kernel, cuts, space), out_shape=jax.Shap...]
where the time goes in v4:
time: 42.1 us; the launch traced here: 41.8 us
  Pallas kernels  38.2 us (91%)
  local copies, waits for them, and re-layouts  3.57 us (8%)
    pallas_call x1, Pallas kernels, local(): pl.pallas_call(functools.partial(kernel, cuts, space), out_shape=jax.Shap...  38.2 us
    unnamed x6, local copies, waits for them, and re-layouts  2.18 us

profile of v4, /device:TPU:26, one launch (start us, length us, event | category | flops | bytes accessed | tf_op | source)
XLA Modules:
  0.0 41.8 jit_solution(5097746916198645400)
XLA Ops:
  0.0 0.7 %reshape.10.pipe_ref = s32[4,512]{1,0:T(4,128)S(1)} reshape(s32[2048]{0:T(1024)} %param.8) | data formatting | bytes 16384 | tf_op jit(solution)/shard_map/reshape | solution.py:300
  0.7 0.0 copy-start
  0.7 0.8 %copy-done = f32[1,16,2,512]{3,2,1,0:T(2,128)S(1)} copy-done((f32[1,16,2,512]{3,2,1,0:T(2,128)S(1)}, f32[1,16,2,512]{3,2,1,0:T(2,128)}, u32[]{:S(2)}) %copy-start) | copy-done | bytes 65560
  1.5 0.0 copy-start.1
  1.5 0.7 %copy-done.1 = f32[1,2,512]{2,1,0:T(2,128)S(1)} copy-done((f32[1,2,512]{2,1,0:T(2,128)S(1)}, f32[1,2,512]{2,1,0:T(2,128)}, u32[]{:S(2)}) %copy-start.1) | copy-done | bytes 4120
  2.2 0.0 copy-start.2
  2.2 0.7 %copy-done.2 = f32[128]{0:T(128)S(1)} copy-done((f32[128]{0:T(128)S(1)}, f32[128]{0:T(128)}, u32[]{:S(2)}) %copy-start.2) | copy-done | bytes 536
  2.9 38.2 %shard_map.55 = f32[16,1024]{1,0:T(8,128)S(1)} custom-call(f32[1,16,2,512]{3,2,1,0:T(2,128)S(1)} %copy-done, f32[1,2,512]{2,1,0:T(2,128)S(1)} %copy-done.1, bf16[1024,2,2048]{2,1,0:T(2,128)(2,1)} %bitcast.1, s32[4,512]{1,0:T(4,128)S(1)} %reshape.10.pipe_ref, f32[128]{0:T(128)S(1)} %copy-done.2), custom_call_target="tpu_custom_call" | custom-call | tf_op jit(solution)/shard_map/pallas_call | solution.py:304
  41.1 0.7 %reshape.11 = f32[1,16,2,512]{3,2,1,0:T(2,128)} reshape(f32[16,1024]{1,0:T(8,128)S(1)} %shard_map.55) | data formatting | bytes 131072 | tf_op jit(solution)/shard_map/reshape | solution.py:335
Async XLA Ops:
  0.7 0.8 %copy-start = (f32[1,16,2,512]{3,2,1,0:T(2,128)S(1)}, f32[1,16,2,512]{3,2,1,0:T(2,128)}, u32[]{:S(2)}) copy-start(f32[1,16,2,512]{3,2,1,0:T(2,128)} %x_ref.1) | copy-start | bytes 196612
  1.5 0.7 %copy-start.1 = (f32[1,2,512]{2,1,0:T(2,128)S(1)}, f32[1,2,512]{2,1,0:T(2,128)}, u32[]{:S(2)}) copy-start(f32[1,2,512]{2,1,0:T(2,128)} %scl_ref.1) | copy-start | bytes 12292
  2.2 0.7 %copy-start.2 = (f32[128]{0:T(128)S(1)}, f32[128]{0:T(128)}, u32[]{:S(2)}) copy-start(f32[128]{0:T(128)} %fric_ref.1) | copy-start | bytes 1540
